TPU v7x, 256 devices: a whole 4x4x8 slice. The times are simulated.
256 devices in a mesh: member: 32 (over z_hi, x, y), row: 8 (over z_lo, core).
Axes of the slice: x: 4, y: 4, z: 8 (z_hi: 2, z_lo: 4; z = z_hi * 4 + z_lo), core: 2. Of those that a mesh axis runs over, the one named last changes fastest.
Arguments:
- fields: float32 [64, 3, 128, 1024], P('member', None, 'row'), may hold values from -1.5 to 1.5
- bathymetry: int32 [128, 1024], P('row'), may hold values from 250 to 300
- copy_lists: int32 [3, 6, 64], replicated, may hold values from 0 to 63, as said below
Outputs:
- final_fields: float32 [64, 3, 128, 1024], P('member', None, 'row')
Inputs may be any that keep to these rules, and one draw needn't show every extreme that they name: copy_lists[c, s, m] is m or m xor 2 to the power s; members m and m xor 2 to the power s either both keep their own state or both take the same one of the two.
All inputs are finite; a program needn't handle non-finite values.
Results may differ from a plain program's by a relative error of at most 0.00002.
Values sent between devices are 32-bit elements; how exact they have to be, the bound alone decides.
No kernel may reach another device: no remote copies, remote signals or barrier semaphores. Data moves between devices by JAX's collectives and lax.ppermute only.
A program may use at most 64 MiB of HBM per device.

v0:
```python
import functools

import jax
import jax.numpy as jnp
from jax import lax
from jax.experimental import pallas as pl
from jax.experimental.pallas import tpu as pltpu
from jax.sharding import PartitionSpec as P

STEPS = 4
HALO = 2 * STEPS
LANES = 128
SUBLANES = 8
HEIGHT_UNIT = 2.0**-5
SPEED_UNIT = 2.0**-3

gravity = 2.0
coriolis = 0.1
friction = 0.02
time_step = 0.25


def turn(x, shift, axis):
    return pltpu.roll(x, shift % x.shape[axis], axis)


def euler(h, u, v, depth, joined):
    keep = 1.0 - time_step * friction
    cross = time_step * coriolis
    column = each(lambda a, b: a + b, depth, h)
    flux_x = each(lambda a, b: a * b, column, u)
    flux_y = each(lambda a, b: a * b, column, v)
    next_h = each(lambda a, b, c: a - (b + c), h, along(flux_x, joined), across(flux_y))
    next_u = each(lambda a, b, c: (keep * a + cross * b) - c, u, v, along(h, joined))
    next_v = each(lambda a, b, c: (keep * b - cross * a) - c, u, v, across(h))
    return next_h, next_u, next_v


def each(f, *grids):
    return [[f(*values) for values in zip(*rows)] for rows in zip(*grids)]


def across(x):
    above = [[turn(y, 1, 0) for y in x[-1]]] + x[:-1]
    below = x[1:] + [[turn(y, -1, 0) for y in x[0]]]
    return each(lambda a, b: b - a, above, below)


def along(x, joined):
    left = each(lambda y: turn(y, 1, 1), x)
    right = each(lambda y: turn(y, -1, 1), x)
    if joined:
        lane = lax.broadcasted_iota(jnp.int32, x[0][0].shape, 1)
        left = [[jnp.where(lane == 0, a, b) for a, b in zip([y[-1]] + y[:-1], y)] for y in left]
        right = [[jnp.where(lane == LANES - 1, a, b) for a, b in zip(y[1:] + [y[0]], y)] for y in right]
    return each(lambda a, b: b - a, left, right)


def one_step(state, depth, joined):
    ahead = euler(*euler(*state, depth, joined), depth, joined)
    return [each(lambda a, b: 0.5 * (a + b), x, y) for x, y in zip(state, ahead)]


def source_of(lists, cycles, sections, members, m):
    for section in range(cycles * sections - 1, -1, -1):
        m = lists[section * members + m]
    return m


def edge_kernel(fields, bathymetry, top, bottom):
    count, parts, rows, width = fields.shape
    for m in range(count):
        for f in range(parts):
            unit = HEIGHT_UNIT if f == 0 else SPEED_UNIT
            top[m * parts + f] = unit * fields[m, f, 0:HALO]
            bottom[m * parts + f] = unit * fields[m, f, rows - HALO : rows]
    depth = scaled_depth(bathymetry[...])
    top[count * parts] = depth[0:HALO]
    bottom[count * parts] = depth[rows - HALO :]


def scaled_depth(hundredths):
    return hundredths.astype(jnp.float32) * (0.01 * HEIGHT_UNIT)


def spread(ref, *index):
    ways = ref.shape[-2] // SUBLANES
    return [ref[(*index, pl.ds(q, SUBLANES, stride=ways), slice(None))] for q in range(ways)]


def unspread(ref, values, *index):
    for q, value in enumerate(values):
        ref[(*index, pl.ds(q, SUBLANES, stride=len(values)), slice(None))] = value


def take_cycle(depth, state):
    count, parts, blocks = state.shape[:3]

    def grid(ref, *index):
        return [list(x) for x in zip(*[spread(ref, *index, k) for k in range(blocks)])]

    def step(i, carry):
        m = i // STEPS
        result = one_step([grid(state, m, f) for f in range(parts)], grid(depth), True)
        for f in range(parts):
            for k in range(blocks):
                unspread(state, [x[k] for x in result[f]], m, f, k)
        return carry

    lax.fori_loop(0, count * STEPS, step, 0)


def fill(state, up, top, bottom, down):
    count, parts, blocks = state.shape[:3]
    for m in range(count):
        for f in range(parts):
            for i, piece in enumerate((up, top, bottom, down)):
                rows = piece(m, f)
                for k in range(blocks):
                    state[m, f, k, HALO * i : HALO * (i + 1)] = rows[:, LANES * k : LANES * (k + 1)]


def put_edges(state, top, bottom):
    count, parts, blocks = state.shape[:3]
    for m in range(count):
        for f in range(parts):
            for k in range(blocks):
                for i, ref in enumerate((top, bottom)):
                    piece = state[m, f, k, HALO * (i + 1) : HALO * (i + 2)]
                    ref[m * parts + f, :, LANES * k : LANES * (k + 1)] = piece


def plane(ref):
    return lambda m, f: ref[3 * m + f]


def first_kernel(fields, bathymetry, up, down, top, bottom, depth, state):
    count, parts, rows, width = fields.shape
    own = scaled_depth(bathymetry[...])
    pieces = (up[count * parts], own[:HALO], own[HALO:], down[count * parts])
    for i, piece in enumerate(pieces):
        for k in range(width // LANES):
            depth[k, HALO * i : HALO * (i + 1)] = piece[:, LANES * k : LANES * (k + 1)]

    def part(first):
        def rows_of(m, f):
            return (HEIGHT_UNIT if f == 0 else SPEED_UNIT) * fields[m, f, first : first + HALO]

        return rows_of

    fill(state, plane(up), part(0), part(HALO), plane(down))
    take_cycle(depth, state)
    put_edges(state, top, bottom)


def middle_kernel(depth, up, own_top, own_bottom, down, top, bottom, state):
    fill(state, plane(up), plane(own_top), plane(own_bottom), plane(down))
    take_cycle(depth, state)
    put_edges(state, top, bottom)


def last_kernel(depth, up, own_top, own_bottom, down, packed, state):
    fill(state, plane(up), plane(own_top), plane(own_bottom), plane(down))
    take_cycle(depth, state)
    count, parts, blocks = state.shape[:3]
    ways = packed.shape[0] // blocks
    stride = LANES // ways
    group = lax.broadcasted_iota(jnp.int32, (HALO, LANES), 1) // stride
    for f in range(parts):
        for k in range(blocks):
            pieces = [state[m, f, k, HALO * (t + 1) : HALO * (t + 2)] for t in range(2) for m in range(count)]
            for j in range(ways):
                total = None
                for i, piece in enumerate(pieces):
                    moved = turn(piece, stride * (i - j), 1)
                    total = moved if total is None else jnp.where(group == i, moved, total)
                packed[ways * k + j, f] = total


def gather_kernel(cycles, sections, members, stride, lists, before, after):
    parts = before.shape[1]
    member = lax.broadcasted_iota(jnp.int32, before.shape[2:], 1) // stride & 1

    def one(pair, carry):
        halves = []
        for half in range(2):
            source = source_of(lists, cycles, sections, members, 2 * pair + half)
            shift = (stride * (half - (source & 1))) & (LANES - 1)
            halves.append([pltpu.roll(before[source >> 1, f], shift, 1) for f in range(parts)])
        for f in range(parts):
            after[pair, f] = jnp.where(member == 0, halves[0][f], halves[1][f])
        return carry

    lax.fori_loop(0, members // 2, one, 0, unroll=4)


def unpack_kernel(stride, arrived, out):
    ways = LANES // stride
    group = lax.broadcasted_iota(jnp.int32, (HALO, LANES), 1) // stride
    for f in range(3):
        unit = 1 / (HEIGHT_UNIT if f == 0 else SPEED_UNIT)
        for k in range(arrived.shape[0] // ways):
            pieces = [unit * arrived[ways * k + j, f] for j in range(ways)]
            for tile in range(2):
                for half in range(2):
                    place = 2 * tile + half
                    total = None
                    for j in range(ways):
                        piece = turn(pieces[j], stride * (j - place), 1)
                        total = piece if total is None else jnp.where(group == j, piece, total)
                    out[half, f, HALO * tile : HALO * (tile + 1), LANES * k : LANES * (k + 1)] = total


def body(fields, bathymetry, copy_lists):
    count, parts, rows, width = fields.shape
    devices = lax.axis_size("member")
    members = count * devices
    cycles, sections = copy_lists.shape[:2]
    ring = lax.axis_size("row")
    up_route = [(i, (i + 1) % ring) for i in range(ring)]
    down_route = [(j, i) for i, j in up_route]
    vmem = pl.BlockSpec(memory_space=pltpu.VMEM)
    smem = pl.BlockSpec(memory_space=pltpu.SMEM)
    f32 = functools.partial(jax.ShapeDtypeStruct, dtype=jnp.float32)
    tall = rows + 2 * HALO
    state = pltpu.VMEM((count, parts, width // LANES, tall, LANES), jnp.float32)
    columns = f32((devices, parts, HALO, LANES))

    def call(kernel, out_shape, *args, scratch=(), scalars=0, name=None):
        many = isinstance(out_shape, tuple)
        return pl.pallas_call(
            kernel,
            out_shape=out_shape,
            in_specs=[smem] * scalars + [vmem] * (len(args) - scalars),
            out_specs=(vmem,) * len(out_shape) if many else vmem,
            scratch_shapes=scratch,
            compiler_params=pltpu.CompilerParams(vmem_limit_bytes=16 << 20),
            name=name,
        )(*args)

    def exchange(top, bottom):
        return lax.ppermute(bottom, "row", up_route), lax.ppermute(top, "row", down_route)

    line = f32((count * parts + 1, HALO, width))
    up, down = exchange(*call(edge_kernel, (line, line), fields, bathymetry, name="edge"))
    line = f32((count * parts, HALO, width))
    top, bottom, depth = call(
        first_kernel,
        (line, line, f32((width // LANES, tall, LANES))),
        fields,
        bathymetry,
        up,
        down,
        scratch=[state],
        name="first",
    )
    for _ in range(cycles - 2):
        up, down = exchange(top, bottom)
        top, bottom = call(
            middle_kernel, (line, line), depth, up, top, bottom, down, scratch=[state], name="middle"
        )
    up, down = exchange(top, bottom)
    packed = call(last_kernel, columns, depth, up, top, bottom, down, scratch=[state], name="last")

    own = lax.all_to_all(packed, "member", 0, 0, tiled=True)
    chosen = call(
        functools.partial(gather_kernel, cycles, sections, members, width // devices),
        columns,
        copy_lists.reshape(-1),
        own,
        scalars=1,
        name="gather",
    )
    arrived = lax.all_to_all(chosen, "member", 0, 0, tiled=True)
    return call(
        functools.partial(unpack_kernel, width // devices), f32(fields.shape), arrived, name="unpack"
    )


def solution(mesh):
    placed = (P("member", None, "row", None), P("row", None), P())
    return jax.shard_map(
        body, mesh=mesh, in_specs=placed, out_specs=P("member", None, "row", None), check_vma=False
    )
```

profile of v0, /device:TPU:2, one launch (start us, length us, event | category | flops | bytes accessed | tf_op | source)
XLA Modules:
  0.0 89.9 jit_solution(1918193265489644415)
XLA Ops:
  0.0 0.0 copy-start
  0.0 1.0 %copy-done = f32[2,3,16,1024]{3,2,1,0:T(8,128)S(1)} copy-done((f32[2,3,16,1024]{3,2,1,0:T(8,128)S(1)}, f32[2,3,16,1024]{3,2,1,0:T(8,128)}, u32[]{:S(2)}) %copy-start) | copy-done | bytes 393240
  1.0 0.0 copy-start.1
  1.0 0.8 copy-done.1
  1.9 0.1 collective-permute-start
  2.0 4.1 %collective-permute-start.1 = (f32[7,8,1024]{2,1,0:T(8,128)S(1)}, f32[7,8,1024]{2,1,0:T(8,128)S(1)}, u32[]{:S(2)}, u32[]{:S(2)}) collective-permute-start(f32[7,8,1024]{2,1,0:T(8,128)S(1)} %get-tuple-element.13), channel_id=1, source_target_pairs={{1,0},{2,1},{3,2},{4,3},{5,4},{6,5},{7,6},{0,7},{9,8},{10,9},{11,1... | collective-permute-start | bytes 688136 | tf_op jit(solution)/shard_map/ppermute | solution.py:242
  6.1 3.8 %collective-permute-done.up = f32[7,8,1024]{2,1,0:T(8,128)S(1)} collective-permute-done((f32[7,8,1024]{2,1,0:T(8,128)S(1)}, f32[7,8,1024]{2,1,0:T(8,128)S(1)}, u32[]{:S(2)}, u32[]{:S(2)}) %collective-permute-start) | collective-permute-done | bytes 229408 | tf_op jit(solution)/shard_map/ppermute | solution.py:242
  9.9 0.0 collective-permute-done.1.down
  9.9 3.7 %first.1 = (f32[6,8,1024]{2,1,0:T(8,128)S(1)}, f32[6,8,1024]{2,1,0:T(8,128)S(1)}, f32[8,32,128]{2,1,0:T(8,128)S(1)}) custom-call(f32[2,3,16,1024]{3,2,1,0:T(8,128)S(1)} %copy-done, s32[16,1024]{1,0:T(8,128)S(1)} %copy-done.1, f32[7,8,1024]{2,1,0:T(8,128)S(1)} %collective-permute-done.up, f32[7,8,1024]{2,1,0:T(8,128)S(1)} %collective-permute-done.1.down), custom_call_target="tpu_custom_call" | custom-call | tf_op jit(solution)/shard_map/first/pallas_call | solution.py:231
  13.6 2.1 %collective-permute-start.2 = (f32[6,8,1024]{2,1,0:T(8,128)S(1)}, f32[6,8,1024]{2,1,0:T(8,128)S(1)}, u32[]{:S(2)}, u32[]{:S(2)}) collective-permute-start(f32[6,8,1024]{2,1,0:T(8,128)S(1)} %get-tuple-element.15.own_bottom), channel_id=1, source_target_pairs={{0,1},{1,2},{2,3},{3,4},{4,5},{5,6},{6,7},{7,0},{8,9},{9,10},{10,1... | collective-permute-start | bytes 589832 | tf_op jit(solution)/shard_map/ppermute | solution.py:242
  15.7 1.7 %collective-permute-start.3 = (f32[6,8,1024]{2,1,0:T(8,128)S(1)}, f32[6,8,1024]{2,1,0:T(8,128)S(1)}, u32[]{:S(2)}, u32[]{:S(2)}) collective-permute-start(f32[6,8,1024]{2,1,0:T(8,128)S(1)} %get-tuple-element.16.own_top), channel_id=1, source_target_pairs={{1,0},{2,1},{3,2},{4,3},{5,4},{6,5},{7,6},{0,7},{9,8},{10,9},{11,1... | collective-permute-start | bytes 589832 | tf_op jit(solution)/shard_map/ppermute | solution.py:242
  17.3 3.4 %collective-permute-done.2.up = f32[6,8,1024]{2,1,0:T(8,128)S(1)} collective-permute-done((f32[6,8,1024]{2,1,0:T(8,128)S(1)}, f32[6,8,1024]{2,1,0:T(8,128)S(1)}, u32[]{:S(2)}, u32[]{:S(2)}) %collective-permute-start.2) | collective-permute-done | bytes 196640 | tf_op jit(solution)/shard_map/ppermute | solution.py:242
  20.7 0.0 collective-permute-done.3.down
  20.7 3.7 %middle.1 = (f32[6,8,1024]{2,1,0:T(8,128)S(1)}, f32[6,8,1024]{2,1,0:T(8,128)S(1)}) custom-call(f32[8,32,128]{2,1,0:T(8,128)S(1)} %get-tuple-element.14.depth, f32[6,8,1024]{2,1,0:T(8,128)S(1)} %collective-permute-done.2.up, f32[6,8,1024]{2,1,0:T(8,128)S(1)} %get-tuple-element.16.own_top, f32[6,8,1024]{2,1,0:T(8,128)S(1)} %get-tuple-element.15.own_bottom, ...), custom_call_target="tpu_custom_call" | custom-call | tf_op jit(solution)/shard_map/middle/pallas_call | solution.py:231
  24.4 1.9 %collective-permute-start.4 = (f32[6,8,1024]{2,1,0:T(8,128)S(1)}, f32[6,8,1024]{2,1,0:T(8,128)S(1)}, u32[]{:S(2)}, u32[]{:S(2)}) collective-permute-start(f32[6,8,1024]{2,1,0:T(8,128)S(1)} %get-tuple-element.17.own_bottom), channel_id=1, source_target_pairs={{0,1},{1,2},{2,3},{3,4},{4,5},{5,6},{6,7},{7,0},{8,9},{9,10},{10,1... | collective-permute-start | bytes 589832 | tf_op jit(solution)/shard_map/ppermute | solution.py:242
  26.3 1.9 %collective-permute-start.5 = (f32[6,8,1024]{2,1,0:T(8,128)S(1)}, f32[6,8,1024]{2,1,0:T(8,128)S(1)}, u32[]{:S(2)}, u32[]{:S(2)}) collective-permute-start(f32[6,8,1024]{2,1,0:T(8,128)S(1)} %get-tuple-element.18.own_top), channel_id=1, source_target_pairs={{1,0},{2,1},{3,2},{4,3},{5,4},{6,5},{7,6},{0,7},{9,8},{10,9},{11,1... | collective-permute-start | bytes 589832 | tf_op jit(solution)/shard_map/ppermute | solution.py:242
  28.2 3.4 %collective-permute-done.4.up = f32[6,8,1024]{2,1,0:T(8,128)S(1)} collective-permute-done((f32[6,8,1024]{2,1,0:T(8,128)S(1)}, f32[6,8,1024]{2,1,0:T(8,128)S(1)}, u32[]{:S(2)}, u32[]{:S(2)}) %collective-permute-start.4) | collective-permute-done | bytes 196640 | tf_op jit(solution)/shard_map/ppermute | solution.py:242
  31.6 0.0 collective-permute-done.5.down
  31.6 4.8 %last.1 = f32[32,3,8,128]{3,2,1,0:T(8,128)} custom-call(f32[8,32,128]{2,1,0:T(8,128)S(1)} %get-tuple-element.14.depth, f32[6,8,1024]{2,1,0:T(8,128)S(1)} %collective-permute-done.4.up, f32[6,8,1024]{2,1,0:T(8,128)S(1)} %get-tuple-element.18.own_top, f32[6,8,1024]{2,1,0:T(8,128)S(1)} %get-tuple-element.17.own_bottom, ...), custom_call_target="tpu_custom_call" | custom-call | tf_op jit(solution)/shard_map/last/pallas_call | solution.py:231
  36.4 0.0 copy-start.2
  36.4 18.2 %all-to-all-start = ((f32[32,3,8,128]{3,2,1,0:T(8,128)}), f32[32,3,8,128]{3,2,1,0:T(8,128)S(1)}, u32[]{:S(2)}, u32[]{:S(2)}) async-start(f32[32,3,8,128]{3,2,1,0:T(8,128)} %last.1), calls=%async_computation | async-start | bytes 786432 | tf_op jit(solution)/shard_map/all_to_all | solution.py:265
  54.6 0.0 copy-done.2
  54.6 0.1 reshape.3.lists
  54.7 12.2 %all-to-all-done.before = f32[32,3,8,128]{3,2,1,0:T(8,128)S(1)} async-done(((f32[32,3,8,128]{3,2,1,0:T(8,128)}), f32[32,3,8,128]{3,2,1,0:T(8,128)S(1)}, u32[]{:S(2)}, u32[]{:S(2)}) %all-to-all-start) | async-done | bytes 393248 | tf_op jit(solution)/shard_map/all_to_all | solution.py:265
  66.9 1.8 %gather.1 = f32[32,3,8,128]{3,2,1,0:T(8,128)S(1)} custom-call(s32[1152]{0:T(1024)S(1)} %reshape.3.lists, f32[32,3,8,128]{3,2,1,0:T(8,128)S(1)} %all-to-all-done.before), custom_call_target="tpu_custom_call" | custom-call | tf_op jit(solution)/shard_map/gather/pallas_call | solution.py:231
  68.7 20.1 %all_to_all.10.arrived = f32[32,3,8,128]{3,2,1,0:T(8,128)S(1)} all-to-all(f32[32,3,8,128]{3,2,1,0:T(8,128)S(1)} %gather.1), channel_id=1, replica_groups=mesh['member'=32,'row'=8] {'member'}, dimensions={0} | all-to-all | bytes 786432 | tf_op jit(solution)/shard_map/all_to_all | solution.py:274
  88.8 1.1 %unpack.1 = f32[2,3,16,1024]{3,2,1,0:T(8,128)} custom-call(f32[32,3,8,128]{3,2,1,0:T(8,128)S(1)} %all_to_all.10.arrived), custom_call_target="tpu_custom_call" | custom-call | tf_op jit(solution)/shard_map/unpack/pallas_call | solution.py:231
  (1 shorter events, 0.0 us)
Async XLA Ops:
  0.0 1.0 %copy-start = (f32[2,3,16,1024]{3,2,1,0:T(8,128)S(1)}, f32[2,3,16,1024]{3,2,1,0:T(8,128)}, u32[]{:S(2)}) copy-start(f32[2,3,16,1024]{3,2,1,0:T(8,128)} %fields.3) | copy-start | bytes 1179652
  1.0 0.8 copy-start.1
  1.9 8.0 %collective-permute-start = (f32[7,8,1024]{2,1,0:T(8,128)S(1)}, f32[7,8,1024]{2,1,0:T(8,128)S(1)}, u32[]{:S(2)}, u32[]{:S(2)}) collective-permute-start(f32[7,8,1024]{2,1,0:T(8,128)S(1)} %get-tuple-element.12), channel_id=1, source_target_pairs={{0,1},{1,2},{2,3},{3,4},{4,5},{5,6},{6,7},{7,0},{8,9},{9,10},{10,1... | collective-permute-start | bytes 688136 | tf_op jit(solution)/shard_map/ppermute | solution.py:242
  2.0 7.9 %collective-permute-start.1 = (f32[7,8,1024]{2,1,0:T(8,128)S(1)}, f32[7,8,1024]{2,1,0:T(8,128)S(1)}, u32[]{:S(2)}, u32[]{:S(2)}) collective-permute-start(f32[7,8,1024]{2,1,0:T(8,128)S(1)} %get-tuple-element.13), channel_id=1, source_target_pairs={{1,0},{2,1},{3,2},{4,3},{5,4},{6,5},{7,6},{0,7},{9,8},{10,9},{11,1... | collective-permute-start | bytes 688136 | tf_op jit(solution)/shard_map/ppermute | solution.py:242
  13.6 7.1 %collective-permute-start.2 = (f32[6,8,1024]{2,1,0:T(8,128)S(1)}, f32[6,8,1024]{2,1,0:T(8,128)S(1)}, u32[]{:S(2)}, u32[]{:S(2)}) collective-permute-start(f32[6,8,1024]{2,1,0:T(8,128)S(1)} %get-tuple-element.15.own_bottom), channel_id=1, source_target_pairs={{0,1},{1,2},{2,3},{3,4},{4,5},{5,6},{6,7},{7,0},{8,9},{9,10},{10,1... | collective-permute-start | bytes 589832 | tf_op jit(solution)/shard_map/ppermute | solution.py:242
  15.7 5.0 %collective-permute-start.3 = (f32[6,8,1024]{2,1,0:T(8,128)S(1)}, f32[6,8,1024]{2,1,0:T(8,128)S(1)}, u32[]{:S(2)}, u32[]{:S(2)}) collective-permute-start(f32[6,8,1024]{2,1,0:T(8,128)S(1)} %get-tuple-element.16.own_top), channel_id=1, source_target_pairs={{1,0},{2,1},{3,2},{4,3},{5,4},{6,5},{7,6},{0,7},{9,8},{10,9},{11,1... | collective-permute-start | bytes 589832 | tf_op jit(solution)/shard_map/ppermute | solution.py:242
  24.4 7.2 %collective-permute-start.4 = (f32[6,8,1024]{2,1,0:T(8,128)S(1)}, f32[6,8,1024]{2,1,0:T(8,128)S(1)}, u32[]{:S(2)}, u32[]{:S(2)}) collective-permute-start(f32[6,8,1024]{2,1,0:T(8,128)S(1)} %get-tuple-element.17.own_bottom), channel_id=1, source_target_pairs={{0,1},{1,2},{2,3},{3,4},{4,5},{5,6},{6,7},{7,0},{8,9},{9,10},{10,1... | collective-permute-start | bytes 589832 | tf_op jit(solution)/shard_map/ppermute | solution.py:242
  26.3 5.3 %collective-permute-start.5 = (f32[6,8,1024]{2,1,0:T(8,128)S(1)}, f32[6,8,1024]{2,1,0:T(8,128)S(1)}, u32[]{:S(2)}, u32[]{:S(2)}) collective-permute-start(f32[6,8,1024]{2,1,0:T(8,128)S(1)} %get-tuple-element.18.own_top), channel_id=1, source_target_pairs={{1,0},{2,1},{3,2},{4,3},{5,4},{6,5},{7,6},{0,7},{9,8},{10,9},{11,1... | collective-permute-start | bytes 589832 | tf_op jit(solution)/shard_map/ppermute | solution.py:242
  36.4 18.2 %copy-start.2 = (s32[3,6,64]{2,1,0:T(8,128)S(1)}, s32[3,6,64]{2,1,0:T(8,128)}, u32[]{:S(2)}) copy-start(s32[3,6,64]{2,1,0:T(8,128)} %param.5) | copy-start | bytes 13828
  36.4 30.5 %all-to-all-start = ((f32[32,3,8,128]{3,2,1,0:T(8,128)}), f32[32,3,8,128]{3,2,1,0:T(8,128)S(1)}, u32[]{:S(2)}, u32[]{:S(2)}) async-start(f32[32,3,8,128]{3,2,1,0:T(8,128)} %last.1), calls=%async_computation | async-start | bytes 786432 | tf_op jit(solution)/shard_map/all_to_all | solution.py:265
where the time goes:
time: 90.2 us; the launch traced here: 89.9 us
  starting transfers between devices  30 us (33%)
  waiting for transfers between devices  22.7 us (25%)
  blocking collectives  20.1 us (22%)
  Pallas kernels  15.2 us (17%)
  local copies, waits for them, and re-layouts  1.91 us (2%)
    all_to_all x1, blocking collectives, body(): arrived = lax.all_to_all(chosen, 'member', 0, 0, tiled=True)  20.1 us
    all_to_all x1, starting transfers between devices, body(): own = lax.all_to_all(packed, 'member', 0, 0, tiled=True)  18.2 us
    pallas_call x6, Pallas kernels, call(): pl.pallas_call(kernel, out_shape=out_shape, in_specs=[smem] * scalars + [...  15.2 us
    all_to_all x1, waiting for transfers between devices, body(): own = lax.all_to_all(packed, 'member', 0, 0, tiled=True)  12.2 us
    ppermute x3, waiting for transfers between devices, exchange(): lax.ppermute(bottom, 'row', up_route)  10.5 us
    ppermute x3, starting transfers between devices, exchange(): lax.ppermute(top, 'row', down_route)  7.69 us
    ppermute x3, starting transfers between devices, exchange(): lax.ppermute(bottom, 'row', up_route)  4.08 us
    unnamed x6, local copies, waits for them, and re-layouts  1.84 us
  transfers between devices with their start and end apart: 7, of which 4 were waited for; matrix products, arithmetic and copies ran while one was open for 0% of the time, Pallas kernels for 0%

commit v1 on v0

v1 whole, which is shorter than its diff:
```python
import functools

import jax
import jax.numpy as jnp
from jax import lax
from jax.experimental import pallas as pl
from jax.experimental.pallas import tpu as pltpu
from jax.sharding import PartitionSpec as P

STEPS = 4
HALO = 2 * STEPS
LANES = 128
SUBLANES = 8
HEIGHT_UNIT = 2.0**-5
SPEED_UNIT = 2.0**-3

gravity = 2.0
coriolis = 0.1
friction = 0.02
time_step = 0.25


def turn(x, shift, axis):
    return pltpu.roll(x, shift % x.shape[axis], axis)


def euler(h, u, v, depth):
    keep = 1.0 - time_step * friction
    cross = time_step * coriolis
    column = each(lambda a, b: a + b, depth, h)
    flux_x = each(lambda a, b: a * b, column, u)
    flux_y = each(lambda a, b: a * b, column, v)
    next_h = each(lambda a, b, c: a - (b + c), h, along(flux_x), across(flux_y))
    next_u = each(lambda a, b, c: (keep * a + cross * b) - c, u, v, along(h))
    next_v = each(lambda a, b, c: (keep * b - cross * a) - c, u, v, across(h))
    return next_h, next_u, next_v


def each(f, *grids):
    return [[f(*values) for values in zip(*rows)] for rows in zip(*grids)]


def across(x):
    above = [[turn(y, 1, 0) for y in x[-1]]] + x[:-1]
    below = x[1:] + [[turn(y, -1, 0) for y in x[0]]]
    return each(lambda a, b: b - a, above, below)


def along(x):
    return [[b - a for a, b in zip([turn(y[-1], 1, 1)] + y[:-1], y[1:] + [turn(y[0], -1, 1)])] for y in x]


def one_step(state, depth):
    ahead = euler(*euler(*state, depth), depth)
    return [each(lambda a, b: 0.5 * (a + b), x, y) for x, y in zip(state, ahead)]


def swap_groups(x):
    x, width = list(x), LANES // len(x)
    group = lax.broadcasted_iota(jnp.int32, x[0].shape, 1) // width
    bit = 1
    while bit < len(x):
        low = group & bit == 0
        for i in range(len(x)):
            if not i & bit:
                a, b = x[i], x[i + bit]
                x[i] = jnp.where(low, a, turn(b, width * bit, 1))
                x[i + bit] = jnp.where(low, turn(a, -width * bit, 1), b)
        bit *= 2
    return x


def pick(x, index):
    return jnp.take_along_axis(x, index, axis=1)


def interleave(x):
    ways = len(x)
    lane = lax.broadcasted_iota(jnp.int32, x[0].shape, 1)
    width = LANES // ways
    return swap_groups([pick(y, ways * (lane % width) + lane // width) for y in x])


def blocks_of(x):
    return [x[:, LANES * k : LANES * (k + 1)] for k in range(x.shape[1] // LANES)]


def offsets(odd):
    return [pl.multiple_of(HALO * x, HALO) for x in (3 * odd, 1 + odd, 2 - odd, 3 - 3 * odd)]


def edge_kernel(odd, fields, bathymetry, *refs):
    count, parts, rows, width = fields.shape
    outs, (held, held_depth, sems) = refs[: 2 * count], refs[2 * count :]
    copies = [pltpu.make_async_copy(bathymetry, held_depth, sems.at[count])]
    copies += [pltpu.make_async_copy(fields.at[m], held.at[m], sems.at[m]) for m in range(count)]
    for copy in copies:
        copy.start()
    _, outer, inner, _ = offsets(odd[0])
    copies[0].wait()
    depth = []
    for first in (outer, inner):
        depth.append(interleave(blocks_of(scaled_depth(held_depth[pl.ds(first - HALO, HALO)]))))
    for m in range(count):
        copies[1 + m].wait()
        for i, first in enumerate((outer, inner)):
            write_blocks(outs[2 * m + i], parts, depth[(i + m) % 2])
            for f in range(parts):
                unit = HEIGHT_UNIT if f == 0 else SPEED_UNIT
                write_blocks(outs[2 * m + i], f, interleave(blocks_of(unit * held[m, f, pl.ds(first - HALO, HALO)])))


def write_blocks(ref, index, values):
    for k, value in enumerate(values):
        ref[index, :, LANES * k : LANES * (k + 1)] = value


def scaled_depth(hundredths):
    return hundredths.astype(jnp.float32) * (0.01 * HEIGHT_UNIT)


def spread(ref, *index):
    ways = ref.shape[-2] // SUBLANES
    return [ref[(*index, pl.ds(q, SUBLANES, stride=ways), slice(None))] for q in range(ways)]


def unspread(ref, values, *index):
    for q, value in enumerate(values):
        ref[(*index, pl.ds(q, SUBLANES, stride=len(values)), slice(None))] = value


def take_steps(depth, state, steps):
    parts, blocks = state.shape[:2]

    def grid(ref, *index):
        return [list(x) for x in zip(*[spread(ref, *index, k) for k in range(blocks)])]

    def step(i, carry):
        result = one_step([grid(state, f) for f in range(parts)], grid(depth))
        for f in range(parts):
            for k in range(blocks):
                unspread(state, [x[k] for x in result[f]], f, k)
        return carry

    lax.fori_loop(0, steps, step, 0)


def fill(place, blocks, pieces):
    for first, piece in pieces:
        for k in range(blocks):
            place(k, pl.ds(first, piece.shape[0]))[...] = piece[:, LANES * k : LANES * (k + 1)]


def plane(ref, f):
    return lambda k, rows: ref.at[f, k, rows]


def first_round(odd, depth, state, tile, pieces):
    parts, blocks = state.shape[:2]
    places = offsets(odd[0])
    for f in range(parts):
        fill(plane(state, f), blocks, [(first, ref[f]) for first, ref in zip(places, pieces)])
    take_steps(depth, state, STEPS)
    for f in range(parts):
        write_blocks(tile, f, [state[f, k, HALO : 3 * HALO] for k in range(blocks)])


def first_kernel(odd, beyond, own_outer, own_inner, beside, tile, depth, state):
    pieces = beyond, own_outer, own_inner, beside
    places = offsets(odd[0])
    parts, blocks = state.shape[:2]
    fill(lambda k, rows: depth.at[k, rows], blocks, [(first, ref[parts]) for first, ref in zip(places, pieces)])
    first_round(odd, depth, state, tile, pieces)


def second_kernel(odd, depth, beyond, own_outer, own_inner, beside, tile, tall_depth, state):
    parts, blocks = state.shape[:2]
    far = pl.multiple_of(5 * HALO * odd[0], HALO)
    near = pl.multiple_of(5 * HALO * (1 - odd[0]), HALO)
    fill(lambda k, rows: tall_depth.at[k, rows], blocks, [(far, beyond[parts]), (near, beside[parts])])
    tall_depth[:, HALO : 5 * HALO] = depth[...]
    first_round(odd, depth, state, tile, (beyond, own_outer, own_inner, beside))


def second_round(odd, depth, state, beyond, own, beside, steps):
    rows = own.shape[1]
    far = pl.multiple_of(2 * rows * odd[0], rows)
    near = pl.multiple_of(2 * rows * (1 - odd[0]), rows)
    for f in range(own.shape[0]):
        fill(plane(state, f), state.shape[1], [(far, beyond[f]), (rows, own[f]), (near, beside[f])])
    take_steps(depth, state, steps)


def third_kernel(steps, odd, depth, beyond, own, beside, tile, state):
    second_round(odd, depth, state, beyond, own, beside, steps)
    parts, blocks = state.shape[:2]
    for f in range(parts):
        write_blocks(tile, f, [state[f, k, 2 * HALO : 4 * HALO] for k in range(blocks)])


def last_kernel(steps, odd, depth, beyond, own, beside, other, packed, state):
    second_round(odd, depth, state, beyond, own, beside, steps)
    parts, blocks = state.shape[:2]
    ways = packed.shape[0] // blocks
    for f in range(parts):
        for k in range(blocks):
            columns = slice(LANES * k, LANES * (k + 1))
            pieces = []
            for i in range(2):
                pieces.append(other[f, HALO * i : HALO * (i + 1), columns])
                pieces.append(state[f, k, HALO * (i + 2) : HALO * (i + 3)])
            for j, value in enumerate(swap_groups(pieces)):
                packed[ways * k + j, f] = value


def source_kernel(lists, sources):
    members = sources.shape[0]

    def one(member, carry):
        source = member
        for section in range(lists.shape[0] // members - 1, -1, -1):
            source = lists[section * members + source]
        sources[member] = source
        return carry

    lax.fori_loop(0, members, one, 0, unroll=16)


def gather_kernel(stride, sources, before, after):
    pairs, parts = before.shape[:2]
    member = lax.broadcasted_iota(jnp.int32, before.shape[2:], 1) // stride & 1

    def one(pair, carry):
        halves = []
        for half in range(2):
            source = sources[2 * pair + half]
            shift = (stride * (half - (source & 1))) & (LANES - 1)
            halves.append([pltpu.roll(before[source >> 1, f], shift, 1) for f in range(parts)])
        for f in range(parts):
            after[pair, f] = jnp.where(member == 0, halves[0][f], halves[1][f])
        return carry

    lax.fori_loop(0, pairs, one, 0, unroll=8)


def unpack_kernel(arrived, out):
    count, parts, rows, width = out.shape
    blocks = width // LANES
    ways = arrived.shape[0] // blocks
    lane = lax.broadcasted_iota(jnp.int32, (HALO, LANES), 1)
    order = LANES // blocks * (lane % blocks) + lane // blocks
    for f in range(parts):
        unit = 1 / (HEIGHT_UNIT if f == 0 else SPEED_UNIT)
        for j in range(ways):
            pieces = swap_groups([unit * arrived[ways * k + j, f] for k in range(blocks)])
            for i, piece in enumerate(pieces):
                half, m, low = i // 4, i // 2 % 2, i % 2
                k = 2 * j + low
                out[m, f, HALO * half : HALO * (half + 1), LANES * k : LANES * (k + 1)] = pick(piece, order)


def body(fields, bathymetry, copy_lists):
    count, parts, rows, width = fields.shape
    devices = lax.axis_size("member")
    cycles = copy_lists.shape[0]
    ring = lax.axis_size("row")
    within = [(i, i ^ 1) for i in range(ring)]
    across_chips = [(i, (i + 1 if i % 2 else i - 1) % ring) for i in range(ring)]
    odd = (lax.axis_index("row") % 2).astype(jnp.int32).reshape(1)
    vmem = pl.BlockSpec(memory_space=pltpu.VMEM)
    smem = pl.BlockSpec(memory_space=pltpu.SMEM)
    f32 = functools.partial(jax.ShapeDtypeStruct, dtype=jnp.float32)
    columns = f32((devices, parts, HALO, LANES))

    def call(kernel, out_shape, *args, scratch=(), scalars=1, space=vmem, grant=16, name=None):
        many = isinstance(out_shape, tuple)
        return pl.pallas_call(
            kernel,
            out_shape=out_shape,
            in_specs=[smem] * scalars + [space] * (len(args) - scalars),
            out_specs=(vmem,) * len(out_shape) if many else vmem,
            scratch_shapes=scratch,
            compiler_params=pltpu.CompilerParams(vmem_limit_bytes=grant << 20),
            name=name,
        )(*args)

    def exchange(outer, inner):
        return lax.ppermute(outer, "row", across_chips), lax.ppermute(inner, "row", within)

    blocks = width // LANES
    half = f32((parts + 1, HALO, width))
    tile = f32((parts, rows, width))
    edges = call(
        edge_kernel,
        (half,) * (2 * count),
        odd,
        fields,
        bathymetry,
        scratch=[
            pltpu.VMEM(fields.shape, fields.dtype),
            pltpu.VMEM(bathymetry.shape, bathymetry.dtype),
            pltpu.SemaphoreType.DMA((count + 1,)),
        ],
        space=pl.BlockSpec(memory_space=pltpu.HBM),
        name="edge",
    )
    now = [edges[2 * m : 2 * m + 2] for m in range(count)]
    around = [exchange(*x) for x in now]
    pieces = [(beyond, *x, beside) for x, (beyond, beside) in zip(now, around)]

    def state(tall):
        return [pltpu.VMEM((parts, blocks, tall, LANES), jnp.float32)]

    tall = rows + 2 * HALO
    first, depth = call(
        first_kernel, (tile, f32((blocks, tall, LANES))), odd, *pieces[0], scratch=state(tall), name="first"
    )
    around = [exchange(first, first)]
    tall = rows * 3
    second, tall_depth = call(
        second_kernel,
        (tile, f32((blocks, tall, LANES))),
        odd,
        depth,
        *pieces[1],
        scratch=state(rows + 2 * HALO),
        name="second",
    )
    around.append(exchange(second, second))
    steps = (cycles - 1) * STEPS
    first = call(
        functools.partial(third_kernel, steps),
        tile,
        odd,
        tall_depth,
        around[0][0],
        first,
        around[0][1],
        scratch=state(tall),
        name="third",
    )
    packed = call(
        functools.partial(last_kernel, steps),
        columns,
        odd,
        tall_depth,
        around[1][0],
        second,
        around[1][1],
        first,
        scratch=state(tall),
        name="last",
    )

    own = lax.all_to_all(packed, "member", 0, 0, tiled=True)
    sources = pl.pallas_call(
        source_kernel,
        out_shape=jax.ShapeDtypeStruct((count * devices,), jnp.int32),
        in_specs=[smem],
        out_specs=smem,
        name="sources",
    )(copy_lists.reshape(-1))
    chosen = call(
        functools.partial(gather_kernel, width // devices), columns, sources, own, name="gather"
    )
    arrived = lax.all_to_all(chosen, "member", 0, 0, tiled=True)
    return call(unpack_kernel, f32(fields.shape), arrived, scalars=0, name="unpack")


def solution(mesh):
    placed = (P("member", None, "row", None), P("row", None), P())
    return jax.shard_map(
        body, mesh=mesh, in_specs=placed, out_specs=P("member", None, "row", None), check_vma=False
    )
```

time: 90.2 us -> 80.9 us (0.90)
  starting transfers between devices: 30 us -> 23.7 us
  waiting for transfers between devices: 22.7 us -> 16.7 us
  local copies, waits for them, and re-layouts: 1.91 us -> 3.08 us
  blocking collectives: 20.1 us -> 21.2 us
    all_to_all x1, starting transfers between devices: 18.2 us -> 13.2 us  [body(): own = lax.all_to_all(packed, 'member', 0, 0, tiled=True)]
    ppermute x6 -> x8, waiting for transfers between devices: 10.5 us -> 5.96 us  [the longest x4 5.95 us: exchange(): lax.ppermute(outer, 'row', across_chips)]
    pallas_call x0 -> x1, Pallas kernels: none -> 2.06 us  [body(): pl.pallas_call(source_kernel, out_shape=jax.ShapeDtypeStruct((count * dev...]
    pallas_call x6 -> x7, Pallas kernels: 15.2 us -> 13.7 us  [call(): pl.pallas_call(kernel, out_shape=out_shape, in_specs=[smem] * scalars + [...]
    all_to_all x1, waiting for transfers between devices: 12.2 us -> 10.8 us  [body(): own = lax.all_to_all(packed, 'member', 0, 0, tiled=True)]
    ppermute x6 -> x8, starting transfers between devices: 11.8 us -> 10.5 us  [the longest x4 10.5 us: exchange(): lax.ppermute(outer, 'row', across_chips)]
    all_to_all x1, blocking collectives: 20.1 us -> 21.2 us  [body(): arrived = lax.all_to_all(chosen, 'member', 0, 0, tiled=True)]
    unnamed x6 -> x8, local copies, waits for them, and re-layouts: 1.84 us -> 2.41 us
  transfers between devices with their start and end apart: 7 -> 9, of which waited for: 4 -> 4; matrix products, arithmetic and copies ran while one was open for 0% -> 1% of each run, Pallas kernels for 0% -> 8%
where the time goes in v1:
time: 80.9 us; the launch traced here: 80.5 us
  starting transfers between devices  23.7 us (29%)
  blocking collectives  21.2 us (26%)
  waiting for transfers between devices  16.7 us (21%)
  Pallas kernels  15.8 us (20%)
  local copies, waits for them, and re-layouts  3.08 us (4%)
    all_to_all x1, blocking collectives, body(): arrived = lax.all_to_all(chosen, 'member', 0, 0, tiled=True)  21.2 us
    pallas_call x7, Pallas kernels, call(): pl.pallas_call(kernel, out_shape=out_shape, in_specs=[smem] * scalars + [...  13.7 us
    all_to_all x1, starting transfers between devices, body(): own = lax.all_to_all(packed, 'member', 0, 0, tiled=True)  13.2 us
    all_to_all x1, waiting for transfers between devices, body(): own = lax.all_to_all(packed, 'member', 0, 0, tiled=True)  10.8 us
    ppermute x4, starting transfers between devices, exchange(): lax.ppermute(outer, 'row', across_chips)  10.5 us
    ppermute x4, waiting for transfers between devices, exchange(): lax.ppermute(outer, 'row', across_chips)  5.95 us
    unnamed x8, local copies, waits for them, and re-layouts  2.41 us
    pallas_call x1, Pallas kernels, body(): pl.pallas_call(source_kernel, out_shape=jax.ShapeDtypeStruct((count * dev...  2.06 us
  transfers between devices with their start and end apart: 9, of which 4 were waited for; matrix products, arithmetic and copies ran while one was open for 1% of the time, Pallas kernels for 8%

profile of v1, /device:TPU:2, one launch (start us, length us, event | category | flops | bytes accessed | tf_op | source)
XLA Modules:
  0.0 80.5 jit_solution(872805820096832570)
XLA Ops:
  0.0 0.0 copy-start
  0.0 1.0 %copy-done = f32[2,3,16,1024]{3,2,1,0:T(8,128)S(1)} copy-done((f32[2,3,16,1024]{3,2,1,0:T(8,128)S(1)}, f32[2,3,16,1024]{3,2,1,0:T(8,128)}, u32[]{:S(2)}) %copy-start) | copy-done | bytes 393240
  1.0 0.0 copy-start.1
  1.0 0.8 %copy-done.1 = s32[16,1024]{1,0:T(8,128)S(1)} copy-done((s32[16,1024]{1,0:T(8,128)S(1)}, s32[16,1024]{1,0:T(8,128)}, u32[]{:S(2)}) %copy-start.1) | copy-done | bytes 65560
  1.8 1.6 %edge.1 = (f32[4,8,1024]{2,1,0:T(8,128)S(1)}, f32[4,8,1024]{2,1,0:T(8,128)S(1)}, f32[4,8,1024]{2,1,0:T(8,128)S(1)}, f32[4,8,1024]{2,1,0:T(8,128)S(1)}) custom-call(s32[1]{0:T(128)} %bitcast.odd, f32[2,3,16,1024]{3,2,1,0:T(8,128)S(1)} %copy-done, s32[16,1024]{1,0:T(8,128)S(1)} %copy-done.1), custom_call_target="tpu_custom_call" | custom-call | tf_op jit(solution)/shard_map/edge/pallas_call | solution.py:277
  3.5 4.2 %collective-permute-start = (f32[4,8,1024]{2,1,0:T(8,128)S(1)}, f32[4,8,1024]{2,1,0:T(8,128)S(1)}, u32[]{:S(2)}, u32[]{:S(2)}) collective-permute-start(f32[4,8,1024]{2,1,0:T(8,128)S(1)} %get-tuple-element.13.own_outer), channel_id=1, source_target_pairs={{0,7},{1,2},{2,1},{3,4},{4,3},{5,6},{6,5},{7,0},{8,15},{9,10},{10,... | collective-permute-start | bytes 393224 | tf_op jit(solution)/shard_map/ppermute | solution.py:288
  7.6 0.0 collective-permute-start.1
  7.6 0.8 collective-permute-start.2
  8.4 0.0 collective-permute-start.3
  8.4 2.9 %collective-permute-done.beyond = f32[4,8,1024]{2,1,0:T(8,128)S(1)} collective-permute-done((f32[4,8,1024]{2,1,0:T(8,128)S(1)}, f32[4,8,1024]{2,1,0:T(8,128)S(1)}, u32[]{:S(2)}, u32[]{:S(2)}) %collective-permute-start) | collective-permute-done | bytes 131104 | tf_op jit(solution)/shard_map/ppermute | solution.py:288
  11.4 0.0 collective-permute-done.1.beside
  11.4 0.9 %first.1 = (f32[3,16,1024]{2,1,0:T(8,128)S(1)}, f32[8,32,128]{2,1,0:T(8,128)S(1)}) custom-call(s32[1]{0:T(128)} %bitcast.odd, f32[4,8,1024]{2,1,0:T(8,128)S(1)} %collective-permute-done.beyond, f32[4,8,1024]{2,1,0:T(8,128)S(1)} %get-tuple-element.13.own_outer, f32[4,8,1024]{2,1,0:T(8,128)S(1)} %get-tuple-element.14.own_inner, ...), custom_call_target="tpu_custom_call" | custom-call | tf_op jit(solution)/shard_map/first/pallas_call | solution.py:277
  12.3 3.8 %collective-permute-start.6 = (f32[3,16,1024]{2,1,0:T(8,128)S(1)}, f32[3,16,1024]{2,1,0:T(8,128)S(1)}, u32[]{:S(2)}, u32[]{:S(2)}) collective-permute-start(f32[3,16,1024]{2,1,0:T(8,128)S(1)} %get-tuple-element.20.own), channel_id=1, source_target_pairs={{0,7},{1,2},{2,1},{3,4},{4,3},{5,6},{6,5},{7,0},{8,15},{9,10},{10,... | collective-permute-start | bytes 589832 | tf_op jit(solution)/shard_map/ppermute | solution.py:288
  16.1 0.0 collective-permute-start.7
  16.1 0.0 collective-permute-done.2.beyond
  16.1 0.0 collective-permute-done.3.beside
  16.1 1.0 %second.1 = (f32[3,16,1024]{2,1,0:T(8,128)S(1)}, f32[8,48,128]{2,1,0:T(8,128)S(1)}) custom-call(s32[1]{0:T(128)} %bitcast.odd, f32[8,32,128]{2,1,0:T(8,128)S(1)} %get-tuple-element.15.depth, f32[4,8,1024]{2,1,0:T(8,128)S(1)} %collective-permute-done.2.beyond, f32[4,8,1024]{2,1,0:T(8,128)S(1)} %get-tuple-element.16.own_outer, ...), custom_call_target="tpu_custom_call" | custom-call | tf_op jit(solution)/shard_map/second/pallas_call | solution.py:277
  17.1 1.7 %collective-permute-start.4 = (f32[3,16,1024]{2,1,0:T(8,128)S(1)}, f32[3,16,1024]{2,1,0:T(8,128)S(1)}, u32[]{:S(2)}, u32[]{:S(2)}) collective-permute-start(f32[3,16,1024]{2,1,0:T(8,128)S(1)} %get-tuple-element.19.own), channel_id=1, source_target_pairs={{0,7},{1,2},{2,1},{3,4},{4,3},{5,6},{6,5},{7,0},{8,15},{9,10},{10,... | collective-permute-start | bytes 589832 | tf_op jit(solution)/shard_map/ppermute | solution.py:288
  18.8 0.0 collective-permute-start.5
  18.8 2.5 %collective-permute-done.6.beyond = f32[3,16,1024]{2,1,0:T(8,128)S(1)} collective-permute-done((f32[3,16,1024]{2,1,0:T(8,128)S(1)}, f32[3,16,1024]{2,1,0:T(8,128)S(1)}, u32[]{:S(2)}, u32[]{:S(2)}) %collective-permute-start.6) | collective-permute-done | bytes 196640 | tf_op jit(solution)/shard_map/ppermute | solution.py:288
  21.3 0.0 collective-permute-done.7.beside
  21.3 2.7 %third.1.other = f32[3,16,1024]{2,1,0:T(8,128)S(1)} custom-call(s32[1]{0:T(128)} %bitcast.odd, f32[8,48,128]{2,1,0:T(8,128)S(1)} %get-tuple-element.18.depth, f32[3,16,1024]{2,1,0:T(8,128)S(1)} %collective-permute-done.6.beyond, f32[3,16,1024]{2,1,0:T(8,128)S(1)} %get-tuple-element.20.own, f32[3,16,1024]{2,1,0:T(8,128)S(1)} %collective-permute-done.7.beside), custom_call_target="tpu_custom_call" | custom-call | tf_op jit(solution)/shard_map/third/pallas_call | solution.py:277
  24.0 0.6 collective-permute-done.4.beyond
  24.6 0.0 collective-permute-done.5.beside
  24.6 4.3 %last.1 = f32[32,3,8,128]{3,2,1,0:T(8,128)} custom-call(s32[1]{0:T(128)} %bitcast.odd, f32[8,48,128]{2,1,0:T(8,128)S(1)} %get-tuple-element.18.depth, f32[3,16,1024]{2,1,0:T(8,128)S(1)} %collective-permute-done.4.beyond, f32[3,16,1024]{2,1,0:T(8,128)S(1)} %get-tuple-element.19.own, f32[3,16,1024]{2,1,0:T(8,128)S(1)} %collective-permute-done.5.beside, ...), custom_call_target="tpu_custom_call" | custom-call | tf_op jit(solution)/shard_map/last/pallas_call | solution.py:277
  28.9 0.0 copy-start.3
  28.9 13.2 %all-to-all-start = ((f32[32,3,8,128]{3,2,1,0:T(8,128)}), f32[32,3,8,128]{3,2,1,0:T(8,128)S(1)}, u32[]{:S(2)}, u32[]{:S(2)}) async-start(f32[32,3,8,128]{3,2,1,0:T(8,128)} %last.1), calls=%async_computation | async-start | bytes 786432 | tf_op jit(solution)/shard_map/all_to_all | solution.py:355
  42.1 0.0 copy-done.3
  42.1 0.7 reshape.6.lists
  42.7 2.1 %sources.1 = s32[64]{0:T(128)} custom-call(s32[1152]{0:T(1024)} %reshape.6.lists), custom_call_target="tpu_custom_call" | custom-call | tf_op jit(solution)/shard_map/sources/pallas_call | solution.py:356
  44.8 10.8 %all-to-all-done.before = f32[32,3,8,128]{3,2,1,0:T(8,128)S(1)} async-done(((f32[32,3,8,128]{3,2,1,0:T(8,128)}), f32[32,3,8,128]{3,2,1,0:T(8,128)S(1)}, u32[]{:S(2)}, u32[]{:S(2)}) %all-to-all-start) | async-done | bytes 393248 | tf_op jit(solution)/shard_map/all_to_all | solution.py:355
  55.6 0.0 copy-start.2
  55.6 0.6 copy-done.2
  56.2 1.0 %gather.1 = f32[32,3,8,128]{3,2,1,0:T(8,128)S(1)} custom-call(s32[64]{0:T(128)S(1)} %copy-done.2, f32[32,3,8,128]{3,2,1,0:T(8,128)S(1)} %all-to-all-done.before), custom_call_target="tpu_custom_call" | custom-call | tf_op jit(solution)/shard_map/gather/pallas_call | solution.py:277
  57.2 21.2 %all_to_all.10.arrived = f32[32,3,8,128]{3,2,1,0:T(8,128)S(1)} all-to-all(f32[32,3,8,128]{3,2,1,0:T(8,128)S(1)} %gather.1), channel_id=1, replica_groups=mesh['member'=32,'row'=8] {'member'}, dimensions={0} | all-to-all | bytes 786432 | tf_op jit(solution)/shard_map/all_to_all | solution.py:366
  78.4 2.1 %unpack.1 = f32[2,3,16,1024]{3,2,1,0:T(8,128)} custom-call(f32[32,3,8,128]{3,2,1,0:T(8,128)S(1)} %all_to_all.10.arrived), custom_call_target="tpu_custom_call" | custom-call | tf_op jit(solution)/shard_map/unpack/pallas_call | solution.py:277
Async XLA Ops:
  0.0 1.0 %copy-start = (f32[2,3,16,1024]{3,2,1,0:T(8,128)S(1)}, f32[2,3,16,1024]{3,2,1,0:T(8,128)}, u32[]{:S(2)}) copy-start(f32[2,3,16,1024]{3,2,1,0:T(8,128)} %fields.1) | copy-start | bytes 1179652
  1.0 0.8 %copy-start.1 = (s32[16,1024]{1,0:T(8,128)S(1)}, s32[16,1024]{1,0:T(8,128)}, u32[]{:S(2)}) copy-start(s32[16,1024]{1,0:T(8,128)} %bathymetry.1) | copy-start | bytes 196612
  3.5 7.9 %collective-permute-start = (f32[4,8,1024]{2,1,0:T(8,128)S(1)}, f32[4,8,1024]{2,1,0:T(8,128)S(1)}, u32[]{:S(2)}, u32[]{:S(2)}) collective-permute-start(f32[4,8,1024]{2,1,0:T(8,128)S(1)} %get-tuple-element.13.own_outer), channel_id=1, source_target_pairs={{0,7},{1,2},{2,1},{3,4},{4,3},{5,6},{6,5},{7,0},{8,15},{9,10},{10,... | collective-permute-start | bytes 393224 | tf_op jit(solution)/shard_map/ppermute | solution.py:288
  7.6 3.7 %collective-permute-start.1 = (f32[4,8,1024]{2,1,0:T(8,128)S(1)}, f32[4,8,1024]{2,1,0:T(8,128)S(1)}, u32[]{:S(2)}, u32[]{:S(2)}) collective-permute-start(f32[4,8,1024]{2,1,0:T(8,128)S(1)} %get-tuple-element.14.own_inner), channel_id=1, source_target_pairs={{0,1},{1,0},{2,3},{3,2},{4,5},{5,4},{6,7},{7,6},{8,9},{9,8},{10,11... | collective-permute-start | bytes 393224 | tf_op jit(solution)/shard_map/ppermute | solution.py:288
  7.6 8.5 %collective-permute-start.2 = (f32[4,8,1024]{2,1,0:T(8,128)S(1)}, f32[4,8,1024]{2,1,0:T(8,128)S(1)}, u32[]{:S(2)}, u32[]{:S(2)}) collective-permute-start(f32[4,8,1024]{2,1,0:T(8,128)S(1)} %get-tuple-element.16.own_outer), channel_id=1, source_target_pairs={{0,7},{1,2},{2,1},{3,4},{4,3},{5,6},{6,5},{7,0},{8,15},{9,10},{10,... | collective-permute-start | bytes 393224 | tf_op jit(solution)/shard_map/ppermute | solution.py:288
  8.4 7.7 %collective-permute-start.3 = (f32[4,8,1024]{2,1,0:T(8,128)S(1)}, f32[4,8,1024]{2,1,0:T(8,128)S(1)}, u32[]{:S(2)}, u32[]{:S(2)}) collective-permute-start(f32[4,8,1024]{2,1,0:T(8,128)S(1)} %get-tuple-element.17.own_inner), channel_id=1, source_target_pairs={{0,1},{1,0},{2,3},{3,2},{4,5},{5,4},{6,7},{7,6},{8,9},{9,8},{10,11... | collective-permute-start | bytes 393224 | tf_op jit(solution)/shard_map/ppermute | solution.py:288
  12.3 9.0 %collective-permute-start.6 = (f32[3,16,1024]{2,1,0:T(8,128)S(1)}, f32[3,16,1024]{2,1,0:T(8,128)S(1)}, u32[]{:S(2)}, u32[]{:S(2)}) collective-permute-start(f32[3,16,1024]{2,1,0:T(8,128)S(1)} %get-tuple-element.20.own), channel_id=1, source_target_pairs={{0,7},{1,2},{2,1},{3,4},{4,3},{5,6},{6,5},{7,0},{8,15},{9,10},{10,... | collective-permute-start | bytes 589832 | tf_op jit(solution)/shard_map/ppermute | solution.py:288
  16.1 5.2 %collective-permute-start.7 = (f32[3,16,1024]{2,1,0:T(8,128)S(1)}, f32[3,16,1024]{2,1,0:T(8,128)S(1)}, u32[]{:S(2)}, u32[]{:S(2)}) collective-permute-start(f32[3,16,1024]{2,1,0:T(8,128)S(1)} %get-tuple-element.20.own), channel_id=1, source_target_pairs={{0,1},{1,0},{2,3},{3,2},{4,5},{5,4},{6,7},{7,6},{8,9},{9,8},{10,11... | collective-permute-start | bytes 589832 | tf_op jit(solution)/shard_map/ppermute | solution.py:288
  17.1 7.5 %collective-permute-start.4 = (f32[3,16,1024]{2,1,0:T(8,128)S(1)}, f32[3,16,1024]{2,1,0:T(8,128)S(1)}, u32[]{:S(2)}, u32[]{:S(2)}) collective-permute-start(f32[3,16,1024]{2,1,0:T(8,128)S(1)} %get-tuple-element.19.own), channel_id=1, source_target_pairs={{0,7},{1,2},{2,1},{3,4},{4,3},{5,6},{6,5},{7,0},{8,15},{9,10},{10,... | collective-permute-start | bytes 589832 | tf_op jit(solution)/shard_map/ppermute | solution.py:288
  18.8 5.7 %collective-permute-start.5 = (f32[3,16,1024]{2,1,0:T(8,128)S(1)}, f32[3,16,1024]{2,1,0:T(8,128)S(1)}, u32[]{:S(2)}, u32[]{:S(2)}) collective-permute-start(f32[3,16,1024]{2,1,0:T(8,128)S(1)} %get-tuple-element.19.own), channel_id=1, source_target_pairs={{0,1},{1,0},{2,3},{3,2},{4,5},{5,4},{6,7},{7,6},{8,9},{9,8},{10,11... | collective-permute-start | bytes 589832 | tf_op jit(solution)/shard_map/ppermute | solution.py:288
  28.9 13.2 %copy-start.3 = (s32[3,6,64]{2,1,0:T(8,128)S(1)}, s32[3,6,64]{2,1,0:T(8,128)}, u32[]{:S(2)}) copy-start(s32[3,6,64]{2,1,0:T(8,128)} %param.5) | copy-start | bytes 13828
  28.9 26.7 %all-to-all-start = ((f32[32,3,8,128]{3,2,1,0:T(8,128)}), f32[32,3,8,128]{3,2,1,0:T(8,128)S(1)}, u32[]{:S(2)}, u32[]{:S(2)}) async-start(f32[32,3,8,128]{3,2,1,0:T(8,128)} %last.1), calls=%async_computation | async-start | bytes 786432 | tf_op jit(solution)/shard_map/all_to_all | solution.py:355
  55.6 0.6 copy-start.2

commit v2 on v1

--- a/solution.py
+++ b/solution.py
@@ -244,19 +244,18 @@
 
 
 def unpack_kernel(arrived, out):
-    count, parts, rows, width = out.shape
+    count, _, rows, width = out.shape
     blocks = width // LANES
     ways = arrived.shape[0] // blocks
     lane = lax.broadcasted_iota(jnp.int32, (HALO, LANES), 1)
     order = LANES // blocks * (lane % blocks) + lane // blocks
-    for f in range(parts):
-        unit = 1 / (HEIGHT_UNIT if f == 0 else SPEED_UNIT)
-        for j in range(ways):
-            pieces = swap_groups([unit * arrived[ways * k + j, f] for k in range(blocks)])
-            for i, piece in enumerate(pieces):
-                half, m, low = i // 4, i // 2 % 2, i % 2
-                k = 2 * j + low
-                out[m, f, HALO * half : HALO * (half + 1), LANES * k : LANES * (k + 1)] = pick(piece, order)
+    unit = jnp.where(pl.program_id(0) == 0, 1 / HEIGHT_UNIT, 1 / SPEED_UNIT)
+    for j in range(ways):
+        pieces = swap_groups([arrived[ways * k + j, 0] for k in range(blocks)])
+        for i, piece in enumerate(pieces):
+            half, m, low = i // 4, i // 2 % 2, i % 2
+            k = 2 * j + low
+            out[m, 0, HALO * half : HALO * (half + 1), LANES * k : LANES * (k + 1)] = unit * pick(piece, order)
 
 
 def body(fields, bathymetry, copy_lists):
@@ -272,7 +271,7 @@
     f32 = functools.partial(jax.ShapeDtypeStruct, dtype=jnp.float32)
     columns = f32((devices, parts, HALO, LANES))
 
-    def call(kernel, out_shape, *args, scratch=(), scalars=1, space=vmem, grant=16, name=None):
+    def call(kernel, out_shape, *args, scratch=(), scalars=1, space=vmem, grant=16 << 20, name=None):
         many = isinstance(out_shape, tuple)
         return pl.pallas_call(
             kernel,
@@ -280,7 +279,7 @@
             in_specs=[smem] * scalars + [space] * (len(args) - scalars),
             out_specs=(vmem,) * len(out_shape) if many else vmem,
             scratch_shapes=scratch,
-            compiler_params=pltpu.CompilerParams(vmem_limit_bytes=grant << 20),
+            compiler_params=pltpu.CompilerParams(vmem_limit_bytes=grant),
             name=name,
         )(*args)
 
@@ -294,8 +293,8 @@
         edge_kernel,
         (half,) * (2 * count),
         odd,
-        fields,
-        bathymetry,
+        pltpu.with_memory_space_constraint(fields, pltpu.HBM),
+        pltpu.with_memory_space_constraint(bathymetry, pltpu.HBM),
         scratch=[
             pltpu.VMEM(fields.shape, fields.dtype),
             pltpu.VMEM(bathymetry.shape, bathymetry.dtype),
@@ -307,6 +306,16 @@
     now = [edges[2 * m : 2 * m + 2] for m in range(count)]
     around = [exchange(*x) for x in now]
     pieces = [(beyond, *x, beside) for x, (beyond, beside) in zip(now, around)]
+
+    sources = pl.pallas_call(
+        source_kernel,
+        out_shape=jax.ShapeDtypeStruct((count * devices,), jnp.int32),
+        in_specs=[smem],
+        out_specs=smem,
+        compiler_params=pltpu.CompilerParams(vmem_limit_bytes=1 << 20),
+        name="sources",
+    )(copy_lists.reshape(-1))
+    pieces[0], sources = lax.optimization_barrier((pieces[0], sources))
 
     def state(tall):
         return [pltpu.VMEM((parts, blocks, tall, LANES), jnp.float32)]
@@ -353,18 +362,19 @@
     )
 
     own = lax.all_to_all(packed, "member", 0, 0, tiled=True)
-    sources = pl.pallas_call(
-        source_kernel,
-        out_shape=jax.ShapeDtypeStruct((count * devices,), jnp.int32),
-        in_specs=[smem],
-        out_specs=smem,
-        name="sources",
-    )(copy_lists.reshape(-1))
     chosen = call(
         functools.partial(gather_kernel, width // devices), columns, sources, own, name="gather"
     )
     arrived = lax.all_to_all(chosen, "member", 0, 0, tiled=True)
-    return call(unpack_kernel, f32(fields.shape), arrived, scalars=0, name="unpack")
+    return pl.pallas_call(
+        unpack_kernel,
+        out_shape=f32(fields.shape),
+        grid=(parts,),
+        in_specs=[pl.BlockSpec((devices, 1, HALO, LANES), lambda f: (0, f, 0, 0))],
+        out_specs=pl.BlockSpec((count, 1, rows, width), lambda f: (0, f, 0, 0)),
+        compiler_params=pltpu.CompilerParams(vmem_limit_bytes=16 << 20),
+        name="unpack",
+    )(arrived)
 
 
 def solution(mesh):

time: 80.9 us -> 77.3 us (0.956)
  blocking collectives: 21.2 us -> 47.4 us
  starting transfers between devices: 23.7 us -> 9.42 us
  waiting for transfers between devices: 16.7 us -> 5.08 us
  local copies, waits for them, and re-layouts: 3.08 us -> 0.07 us
    all_to_all x0 -> x1, blocking collectives: none -> 27.1 us  [body(): own = lax.all_to_all(packed, 'member', 0, 0, tiled=True)]
    all_to_all x1 -> x0, starting transfers between devices: 13.2 us -> none  [body(): own = lax.all_to_all(packed, 'member', 0, 0, tiled=True)]
    all_to_all x1 -> x0, waiting for transfers between devices: 10.8 us -> none  [body(): own = lax.all_to_all(packed, 'member', 0, 0, tiled=True)]
    pallas_call x7 -> x6, Pallas kernels: 13.7 us -> 11.1 us  [call(): pl.pallas_call(kernel, out_shape=out_shape, in_specs=[smem] * scalars + [...]
    unnamed x8 -> x2, local copies, waits for them, and re-layouts: 2.41 us -> 0.01 us
    pallas_call x0 -> x1, Pallas kernels: none -> 1.98 us  [body(): pl.pallas_call(unpack_kernel, out_shape=f32(fields.shape), grid=(parts,),...]
    ppermute x4, starting transfers between devices: 10.5 us -> 9.19 us  [exchange(): lax.ppermute(outer, 'row', across_chips)]
    ppermute x4, waiting for transfers between devices: 5.95 us -> 5.07 us  [exchange(): lax.ppermute(outer, 'row', across_chips)]
  transfers between devices with their start and end apart: 9 -> 8, of which waited for: 4 -> 3; matrix products, arithmetic and copies ran while one was open for 1% -> 0% of each run, Pallas kernels for 8% -> 9%
where the time goes in v2:
time: 77.3 us; the launch traced here: 77.2 us
  blocking collectives  47.4 us (61%)
  Pallas kernels  15.1 us (20%)
  starting transfers between devices  9.42 us (12%)
  waiting for transfers between devices  5.08 us (7%)
    all_to_all x1, blocking collectives, body(): own = lax.all_to_all(packed, 'member', 0, 0, tiled=True)  27.1 us
    all_to_all x1, blocking collectives, body(): arrived = lax.all_to_all(chosen, 'member', 0, 0, tiled=True)  20.3 us
    pallas_call x6, Pallas kernels, call(): pl.pallas_call(kernel, out_shape=out_shape, in_specs=[smem] * scalars + [...  11.1 us
    ppermute x4, starting transfers between devices, exchange(): lax.ppermute(outer, 'row', across_chips)  9.19 us
    ppermute x4, waiting for transfers between devices, exchange(): lax.ppermute(outer, 'row', across_chips)  5.07 us
    pallas_call x1, Pallas kernels, body(): pl.pallas_call(source_kernel, out_shape=jax.ShapeDtypeStruct((count * dev...  2.02 us
    pallas_call x1, Pallas kernels, body(): pl.pallas_call(unpack_kernel, out_shape=f32(fields.shape), grid=(parts,),...  1.98 us
  transfers between devices with their start and end apart: 8, of which 3 were waited for; matrix products, arithmetic and copies ran while one was open for 0% of the time, Pallas kernels for 9%

profile of v2, /device:TPU:2, one launch (start us, length us, event | category | flops | bytes accessed | tf_op | source)
XLA Modules:
  0.0 77.2 jit_solution(10998255037483793325)
XLA Ops:
  0.0 0.0 copy-start
  0.0 1.9 %edge.1 = (f32[4,8,1024]{2,1,0:T(8,128)S(1)}, f32[4,8,1024]{2,1,0:T(8,128)S(1)}, f32[4,8,1024]{2,1,0:T(8,128)S(1)}, f32[4,8,1024]{2,1,0:T(8,128)S(1)}) custom-call(s32[1]{0:T(128)} %bitcast.odd, f32[2,3,16,1024]{3,2,1,0:T(8,128)} %fields.1, s32[16,1024]{1,0:T(8,128)} %bathymetry.1), custom_call_target="tpu_custom_call" | custom-call | tf_op jit(solution)/shard_map/edge/pallas_call | solution.py:276
  1.9 4.2 %collective-permute-start = (f32[4,8,1024]{2,1,0:T(8,128)S(1)}, f32[4,8,1024]{2,1,0:T(8,128)S(1)}, u32[]{:S(2)}, u32[]{:S(2)}) collective-permute-start(f32[4,8,1024]{2,1,0:T(8,128)S(1)} %get-tuple-element.22.own_outer), channel_id=1, source_target_pairs={{0,7},{1,2},{2,1},{3,4},{4,3},{5,6},{6,5},{7,0},{8,15},{9,10},{10,... | collective-permute-start | bytes 393224 | tf_op jit(solution)/shard_map/ppermute | solution.py:287
  6.1 0.0 collective-permute-start.1
  6.1 0.8 %collective-permute-start.2 = (f32[4,8,1024]{2,1,0:T(8,128)S(1)}, f32[4,8,1024]{2,1,0:T(8,128)S(1)}, u32[]{:S(2)}, u32[]{:S(2)}) collective-permute-start(f32[4,8,1024]{2,1,0:T(8,128)S(1)} %get-tuple-element.26.own_outer), channel_id=1, source_target_pairs={{0,7},{1,2},{2,1},{3,4},{4,3},{5,6},{6,5},{7,0},{8,15},{9,10},{10,... | collective-permute-start | bytes 393224 | tf_op jit(solution)/shard_map/ppermute | solution.py:287
  6.9 0.0 collective-permute-start.3
  6.9 0.0 copy-done
  6.9 0.1 reshape.7.lists
  7.0 2.0 %sources.1 = s32[64]{0:T(128)S(1)} custom-call(s32[1152]{0:T(1024)S(1)} %reshape.7.lists), custom_call_target="tpu_custom_call" | custom-call | tf_op jit(solution)/shard_map/sources/pallas_call | solution.py:310
  9.0 0.8 %collective-permute-done.beyond = f32[4,8,1024]{2,1,0:T(8,128)S(1)} collective-permute-done((f32[4,8,1024]{2,1,0:T(8,128)S(1)}, f32[4,8,1024]{2,1,0:T(8,128)S(1)}, u32[]{:S(2)}, u32[]{:S(2)}) %collective-permute-start) | collective-permute-done | bytes 131104 | tf_op jit(solution)/shard_map/ppermute | solution.py:287
  9.8 0.0 collective-permute-done.1.beside
  9.8 0.9 %first.1 = (f32[3,16,1024]{2,1,0:T(8,128)S(1)}, f32[8,32,128]{2,1,0:T(8,128)S(1)}) custom-call(s32[1]{0:T(128)} %bitcast.odd, f32[4,8,1024]{2,1,0:T(8,128)S(1)} %collective-permute-done.beyond, f32[4,8,1024]{2,1,0:T(8,128)S(1)} %get-tuple-element.22.own_outer, f32[4,8,1024]{2,1,0:T(8,128)S(1)} %get-tuple-element.23.own_inner, ...), custom_call_target="tpu_custom_call" | custom-call | tf_op jit(solution)/shard_map/first/pallas_call | solution.py:276
  10.8 3.8 %collective-permute-start.6 = (f32[3,16,1024]{2,1,0:T(8,128)S(1)}, f32[3,16,1024]{2,1,0:T(8,128)S(1)}, u32[]{:S(2)}, u32[]{:S(2)}) collective-permute-start(f32[3,16,1024]{2,1,0:T(8,128)S(1)} %get-tuple-element.30.own), channel_id=1, source_target_pairs={{0,7},{1,2},{2,1},{3,4},{4,3},{5,6},{6,5},{7,0},{8,15},{9,10},{10,... | collective-permute-start | bytes 589832 | tf_op jit(solution)/shard_map/ppermute | solution.py:287
  14.6 0.0 collective-permute-start.7
  14.6 0.0 collective-permute-done.2.beyond
  14.6 0.0 collective-permute-done.3.beside
  14.6 1.0 %second.1 = (f32[3,16,1024]{2,1,0:T(8,128)S(1)}, f32[8,48,128]{2,1,0:T(8,128)S(1)}) custom-call(s32[1]{0:T(128)} %bitcast.odd, f32[8,32,128]{2,1,0:T(8,128)S(1)} %get-tuple-element.25.depth, f32[4,8,1024]{2,1,0:T(8,128)S(1)} %collective-permute-done.2.beyond, f32[4,8,1024]{2,1,0:T(8,128)S(1)} %get-tuple-element.26.own_outer, ...), custom_call_target="tpu_custom_call" | custom-call | tf_op jit(solution)/shard_map/second/pallas_call | solution.py:276
  15.5 0.5 collective-permute-start.4
  16.0 0.2 collective-permute-start.5
  16.2 3.8 %collective-permute-done.6.beyond = f32[3,16,1024]{2,1,0:T(8,128)S(1)} collective-permute-done((f32[3,16,1024]{2,1,0:T(8,128)S(1)}, f32[3,16,1024]{2,1,0:T(8,128)S(1)}, u32[]{:S(2)}, u32[]{:S(2)}) %collective-permute-start.6) | collective-permute-done | bytes 196640 | tf_op jit(solution)/shard_map/ppermute | solution.py:287
  20.0 0.0 collective-permute-done.7.beside
  20.0 2.7 %third.1.other = f32[3,16,1024]{2,1,0:T(8,128)S(1)} custom-call(s32[1]{0:T(128)} %bitcast.odd, f32[8,48,128]{2,1,0:T(8,128)S(1)} %get-tuple-element.28.depth, f32[3,16,1024]{2,1,0:T(8,128)S(1)} %collective-permute-done.6.beyond, f32[3,16,1024]{2,1,0:T(8,128)S(1)} %get-tuple-element.30.own, f32[3,16,1024]{2,1,0:T(8,128)S(1)} %collective-permute-done.7.beside), custom_call_target="tpu_custom_call" | custom-call | tf_op jit(solution)/shard_map/third/pallas_call | solution.py:276
  22.7 0.4 collective-permute-done.4.beyond
  23.2 0.0 collective-permute-done.5.beside
  23.2 3.6 %last.1 = f32[32,3,8,128]{3,2,1,0:T(8,128)S(1)} custom-call(s32[1]{0:T(128)} %bitcast.odd, f32[8,48,128]{2,1,0:T(8,128)S(1)} %get-tuple-element.28.depth, f32[3,16,1024]{2,1,0:T(8,128)S(1)} %collective-permute-done.4.beyond, f32[3,16,1024]{2,1,0:T(8,128)S(1)} %get-tuple-element.29.own, f32[3,16,1024]{2,1,0:T(8,128)S(1)} %collective-permute-done.5.beside, ...), custom_call_target="tpu_custom_call" | custom-call | tf_op jit(solution)/shard_map/last/pallas_call | solution.py:276
  26.7 27.1 %all_to_all.10.before = f32[32,3,8,128]{3,2,1,0:T(8,128)S(1)} all-to-all(f32[32,3,8,128]{3,2,1,0:T(8,128)S(1)} %last.1), channel_id=1, replica_groups=mesh['member'=32,'row'=8] {'member'}, dimensions={0} | all-to-all | bytes 786432 | tf_op jit(solution)/shard_map/all_to_all | solution.py:364
  53.9 1.0 %gather.1 = f32[32,3,8,128]{3,2,1,0:T(8,128)S(1)} custom-call(s32[64]{0:T(128)S(1)} %sources.1, f32[32,3,8,128]{3,2,1,0:T(8,128)S(1)} %all_to_all.10.before), custom_call_target="tpu_custom_call" | custom-call | tf_op jit(solution)/shard_map/gather/pallas_call | solution.py:276
  54.9 20.3 %all_to_all.11.arrived = f32[32,3,8,128]{3,2,1,0:T(8,128)S(1)} all-to-all(f32[32,3,8,128]{3,2,1,0:T(8,128)S(1)} %gather.1), channel_id=1, replica_groups=mesh['member'=32,'row'=8] {'member'}, dimensions={0} | all-to-all | bytes 786432 | tf_op jit(solution)/shard_map/all_to_all | solution.py:368
  75.2 2.0 %unpack.1 = f32[2,3,16,1024]{3,2,1,0:T(8,128)} custom-call(f32[32,3,8,128]{3,2,1,0:T(8,128)S(1)} %all_to_all.11.arrived), custom_call_target="tpu_custom_call" | custom-call | tf_op jit(solution)/shard_map/unpack/pallas_call | solution.py:369
Async XLA Ops:
  0.0 6.9 %copy-start = (s32[3,6,64]{2,1,0:T(8,128)S(1)}, s32[3,6,64]{2,1,0:T(8,128)}, u32[]{:S(2)}) copy-start(s32[3,6,64]{2,1,0:T(8,128)} %param.5) | copy-start | bytes 13828
  1.9 7.9 %collective-permute-start = (f32[4,8,1024]{2,1,0:T(8,128)S(1)}, f32[4,8,1024]{2,1,0:T(8,128)S(1)}, u32[]{:S(2)}, u32[]{:S(2)}) collective-permute-start(f32[4,8,1024]{2,1,0:T(8,128)S(1)} %get-tuple-element.22.own_outer), channel_id=1, source_target_pairs={{0,7},{1,2},{2,1},{3,4},{4,3},{5,6},{6,5},{7,0},{8,15},{9,10},{10,... | collective-permute-start | bytes 393224 | tf_op jit(solution)/shard_map/ppermute | solution.py:287
  6.1 3.7 %collective-permute-start.1 = (f32[4,8,1024]{2,1,0:T(8,128)S(1)}, f32[4,8,1024]{2,1,0:T(8,128)S(1)}, u32[]{:S(2)}, u32[]{:S(2)}) collective-permute-start(f32[4,8,1024]{2,1,0:T(8,128)S(1)} %get-tuple-element.23.own_inner), channel_id=1, source_target_pairs={{0,1},{1,0},{2,3},{3,2},{4,5},{5,4},{6,7},{7,6},{8,9},{9,8},{10,11... | collective-permute-start | bytes 393224 | tf_op jit(solution)/shard_map/ppermute | solution.py:287
  6.1 8.5 %collective-permute-start.2 = (f32[4,8,1024]{2,1,0:T(8,128)S(1)}, f32[4,8,1024]{2,1,0:T(8,128)S(1)}, u32[]{:S(2)}, u32[]{:S(2)}) collective-permute-start(f32[4,8,1024]{2,1,0:T(8,128)S(1)} %get-tuple-element.26.own_outer), channel_id=1, source_target_pairs={{0,7},{1,2},{2,1},{3,4},{4,3},{5,6},{6,5},{7,0},{8,15},{9,10},{10,... | collective-permute-start | bytes 393224 | tf_op jit(solution)/shard_map/ppermute | solution.py:287
  6.9 7.7 %collective-permute-start.3 = (f32[4,8,1024]{2,1,0:T(8,128)S(1)}, f32[4,8,1024]{2,1,0:T(8,128)S(1)}, u32[]{:S(2)}, u32[]{:S(2)}) collective-permute-start(f32[4,8,1024]{2,1,0:T(8,128)S(1)} %get-tuple-element.27.own_inner), channel_id=1, source_target_pairs={{0,1},{1,0},{2,3},{3,2},{4,5},{5,4},{6,7},{7,6},{8,9},{9,8},{10,11... | collective-permute-start | bytes 393224 | tf_op jit(solution)/shard_map/ppermute | solution.py:287
  10.8 9.3 %collective-permute-start.6 = (f32[3,16,1024]{2,1,0:T(8,128)S(1)}, f32[3,16,1024]{2,1,0:T(8,128)S(1)}, u32[]{:S(2)}, u32[]{:S(2)}) collective-permute-start(f32[3,16,1024]{2,1,0:T(8,128)S(1)} %get-tuple-element.30.own), channel_id=1, source_target_pairs={{0,7},{1,2},{2,1},{3,4},{4,3},{5,6},{6,5},{7,0},{8,15},{9,10},{10,... | collective-permute-start | bytes 589832 | tf_op jit(solution)/shard_map/ppermute | solution.py:287
  14.6 5.5 %collective-permute-start.7 = (f32[3,16,1024]{2,1,0:T(8,128)S(1)}, f32[3,16,1024]{2,1,0:T(8,128)S(1)}, u32[]{:S(2)}, u32[]{:S(2)}) collective-permute-start(f32[3,16,1024]{2,1,0:T(8,128)S(1)} %get-tuple-element.30.own), channel_id=1, source_target_pairs={{0,1},{1,0},{2,3},{3,2},{4,5},{5,4},{6,7},{7,6},{8,9},{9,8},{10,11... | collective-permute-start | bytes 589832 | tf_op jit(solution)/shard_map/ppermute | solution.py:287
  15.5 7.6 %collective-permute-start.4 = (f32[3,16,1024]{2,1,0:T(8,128)S(1)}, f32[3,16,1024]{2,1,0:T(8,128)S(1)}, u32[]{:S(2)}, u32[]{:S(2)}) collective-permute-start(f32[3,16,1024]{2,1,0:T(8,128)S(1)} %get-tuple-element.29.own), channel_id=1, source_target_pairs={{0,7},{1,2},{2,1},{3,4},{4,3},{5,6},{6,5},{7,0},{8,15},{9,10},{10,... | collective-permute-start | bytes 589832 | tf_op jit(solution)/shard_map/ppermute | solution.py:287
  16.0 7.2 %collective-permute-start.5 = (f32[3,16,1024]{2,1,0:T(8,128)S(1)}, f32[3,16,1024]{2,1,0:T(8,128)S(1)}, u32[]{:S(2)}, u32[]{:S(2)}) collective-permute-start(f32[3,16,1024]{2,1,0:T(8,128)S(1)} %get-tuple-element.29.own), channel_id=1, source_target_pairs={{0,1},{1,0},{2,3},{3,2},{4,5},{5,4},{6,7},{7,6},{8,9},{9,8},{10,11... | collective-permute-start | bytes 589832 | tf_op jit(solution)/shard_map/ppermute | solution.py:287

commit v3 on v2

--- a/solution.py
+++ b/solution.py
@@ -223,7 +223,7 @@
         sources[member] = source
         return carry
 
-    lax.fori_loop(0, members, one, 0, unroll=16)
+    lax.fori_loop(0, members, one, 0, unroll=64)
 
 
 def gather_kernel(stride, sources, before, after):

time: 77.3 us -> 77.4 us (level)
  transfers between devices with their start and end apart: 8 -> 8, of which waited for: 3 -> 3; matrix products, arithmetic and copies ran while one was open for 0% -> 0% of each run, Pallas kernels for 9% -> 8%
where the time goes in v3:
time: 77.4 us; the launch traced here: 77.2 us
  blocking collectives  47.5 us (61%)
  Pallas kernels  14.9 us (19%)
  starting transfers between devices  9.42 us (12%)
  waiting for transfers between devices  5.18 us (7%)
    all_to_all x1, blocking collectives, body(): own = lax.all_to_all(packed, 'member', 0, 0, tiled=True)  26.8 us
    all_to_all x1, blocking collectives, body(): arrived = lax.all_to_all(chosen, 'member', 0, 0, tiled=True)  20.7 us
    pallas_call x6, Pallas kernels, call(): pl.pallas_call(kernel, out_shape=out_shape, in_specs=[smem] * scalars + [...  11.1 us
    ppermute x4, starting transfers between devices, exchange(): lax.ppermute(outer, 'row', across_chips)  9.2 us
    ppermute x4, waiting for transfers between devices, exchange(): lax.ppermute(outer, 'row', across_chips)  5.17 us
    pallas_call x1, Pallas kernels, body(): pl.pallas_call(unpack_kernel, out_shape=f32(fields.shape), grid=(parts,),...  1.98 us
    pallas_call x1, Pallas kernels, body(): pl.pallas_call(source_kernel, out_shape=jax.ShapeDtypeStruct((count * dev...  1.85 us
  transfers between devices with their start and end apart: 8, of which 3 were waited for; matrix products, arithmetic and copies ran while one was open for 0% of the time, Pallas kernels for 8%

profile of v3, /device:TPU:2, one launch (start us, length us, event | category | flops | bytes accessed | tf_op | source)
XLA Modules:
  0.0 77.2 jit_solution(16941304221726720058)
XLA Ops:
  0.0 0.0 copy-start
  0.0 1.9 %edge.1 = (f32[4,8,1024]{2,1,0:T(8,128)S(1)}, f32[4,8,1024]{2,1,0:T(8,128)S(1)}, f32[4,8,1024]{2,1,0:T(8,128)S(1)}, f32[4,8,1024]{2,1,0:T(8,128)S(1)}) custom-call(s32[1]{0:T(128)} %bitcast.odd, f32[2,3,16,1024]{3,2,1,0:T(8,128)} %fields.1, s32[16,1024]{1,0:T(8,128)} %bathymetry.1), custom_call_target="tpu_custom_call" | custom-call | tf_op jit(solution)/shard_map/edge/pallas_call | solution.py:276
  1.9 4.2 %collective-permute-start = (f32[4,8,1024]{2,1,0:T(8,128)S(1)}, f32[4,8,1024]{2,1,0:T(8,128)S(1)}, u32[]{:S(2)}, u32[]{:S(2)}) collective-permute-start(f32[4,8,1024]{2,1,0:T(8,128)S(1)} %get-tuple-element.22.own_outer), channel_id=1, source_target_pairs={{0,7},{1,2},{2,1},{3,4},{4,3},{5,6},{6,5},{7,0},{8,15},{9,10},{10,... | collective-permute-start | bytes 393224 | tf_op jit(solution)/shard_map/ppermute | solution.py:287
  6.1 0.0 collective-permute-start.1
  6.1 0.8 %collective-permute-start.2 = (f32[4,8,1024]{2,1,0:T(8,128)S(1)}, f32[4,8,1024]{2,1,0:T(8,128)S(1)}, u32[]{:S(2)}, u32[]{:S(2)}) collective-permute-start(f32[4,8,1024]{2,1,0:T(8,128)S(1)} %get-tuple-element.26.own_outer), channel_id=1, source_target_pairs={{0,7},{1,2},{2,1},{3,4},{4,3},{5,6},{6,5},{7,0},{8,15},{9,10},{10,... | collective-permute-start | bytes 393224 | tf_op jit(solution)/shard_map/ppermute | solution.py:287
  6.9 0.0 collective-permute-start.3
  6.9 0.0 copy-done
  6.9 0.1 reshape.7.lists
  7.0 1.9 %sources.1 = s32[64]{0:T(128)S(1)} custom-call(s32[1152]{0:T(1024)S(1)} %reshape.7.lists), custom_call_target="tpu_custom_call" | custom-call | tf_op jit(solution)/shard_map/sources/pallas_call | solution.py:310
  8.8 1.0 %collective-permute-done.beyond = f32[4,8,1024]{2,1,0:T(8,128)S(1)} collective-permute-done((f32[4,8,1024]{2,1,0:T(8,128)S(1)}, f32[4,8,1024]{2,1,0:T(8,128)S(1)}, u32[]{:S(2)}, u32[]{:S(2)}) %collective-permute-start) | collective-permute-done | bytes 131104 | tf_op jit(solution)/shard_map/ppermute | solution.py:287
  9.8 0.0 collective-permute-done.1.beside
  9.8 0.9 %first.1 = (f32[3,16,1024]{2,1,0:T(8,128)S(1)}, f32[8,32,128]{2,1,0:T(8,128)S(1)}) custom-call(s32[1]{0:T(128)} %bitcast.odd, f32[4,8,1024]{2,1,0:T(8,128)S(1)} %collective-permute-done.beyond, f32[4,8,1024]{2,1,0:T(8,128)S(1)} %get-tuple-element.22.own_outer, f32[4,8,1024]{2,1,0:T(8,128)S(1)} %get-tuple-element.23.own_inner, ...), custom_call_target="tpu_custom_call" | custom-call | tf_op jit(solution)/shard_map/first/pallas_call | solution.py:276
  10.8 3.8 %collective-permute-start.6 = (f32[3,16,1024]{2,1,0:T(8,128)S(1)}, f32[3,16,1024]{2,1,0:T(8,128)S(1)}, u32[]{:S(2)}, u32[]{:S(2)}) collective-permute-start(f32[3,16,1024]{2,1,0:T(8,128)S(1)} %get-tuple-element.30.own), channel_id=1, source_target_pairs={{0,7},{1,2},{2,1},{3,4},{4,3},{5,6},{6,5},{7,0},{8,15},{9,10},{10,... | collective-permute-start | bytes 589832 | tf_op jit(solution)/shard_map/ppermute | solution.py:287
  14.6 0.0 collective-permute-start.7
  14.6 0.0 collective-permute-done.2.beyond
  14.6 0.0 collective-permute-done.3.beside
  14.6 1.0 %second.1 = (f32[3,16,1024]{2,1,0:T(8,128)S(1)}, f32[8,48,128]{2,1,0:T(8,128)S(1)}) custom-call(s32[1]{0:T(128)} %bitcast.odd, f32[8,32,128]{2,1,0:T(8,128)S(1)} %get-tuple-element.25.depth, f32[4,8,1024]{2,1,0:T(8,128)S(1)} %collective-permute-done.2.beyond, f32[4,8,1024]{2,1,0:T(8,128)S(1)} %get-tuple-element.26.own_outer, ...), custom_call_target="tpu_custom_call" | custom-call | tf_op jit(solution)/shard_map/second/pallas_call | solution.py:276
  15.5 0.5 collective-permute-start.4
  16.0 0.2 collective-permute-start.5
  16.2 3.7 %collective-permute-done.6.beyond = f32[3,16,1024]{2,1,0:T(8,128)S(1)} collective-permute-done((f32[3,16,1024]{2,1,0:T(8,128)S(1)}, f32[3,16,1024]{2,1,0:T(8,128)S(1)}, u32[]{:S(2)}, u32[]{:S(2)}) %collective-permute-start.6) | collective-permute-done | bytes 196640 | tf_op jit(solution)/shard_map/ppermute | solution.py:287
  19.9 0.0 collective-permute-done.7.beside
  19.9 2.7 %third.1.other = f32[3,16,1024]{2,1,0:T(8,128)S(1)} custom-call(s32[1]{0:T(128)} %bitcast.odd, f32[8,48,128]{2,1,0:T(8,128)S(1)} %get-tuple-element.28.depth, f32[3,16,1024]{2,1,0:T(8,128)S(1)} %collective-permute-done.6.beyond, f32[3,16,1024]{2,1,0:T(8,128)S(1)} %get-tuple-element.30.own, f32[3,16,1024]{2,1,0:T(8,128)S(1)} %collective-permute-done.7.beside), custom_call_target="tpu_custom_call" | custom-call | tf_op jit(solution)/shard_map/third/pallas_call | solution.py:276
  22.7 0.5 collective-permute-done.4.beyond
  23.1 0.0 collective-permute-done.5.beside
  23.1 3.6 %last.1 = f32[32,3,8,128]{3,2,1,0:T(8,128)S(1)} custom-call(s32[1]{0:T(128)} %bitcast.odd, f32[8,48,128]{2,1,0:T(8,128)S(1)} %get-tuple-element.28.depth, f32[3,16,1024]{2,1,0:T(8,128)S(1)} %collective-permute-done.4.beyond, f32[3,16,1024]{2,1,0:T(8,128)S(1)} %get-tuple-element.29.own, f32[3,16,1024]{2,1,0:T(8,128)S(1)} %collective-permute-done.5.beside, ...), custom_call_target="tpu_custom_call" | custom-call | tf_op jit(solution)/shard_map/last/pallas_call | solution.py:276
  26.7 26.8 %all_to_all.10.before = f32[32,3,8,128]{3,2,1,0:T(8,128)S(1)} all-to-all(f32[32,3,8,128]{3,2,1,0:T(8,128)S(1)} %last.1), channel_id=1, replica_groups=mesh['member'=32,'row'=8] {'member'}, dimensions={0} | all-to-all | bytes 786432 | tf_op jit(solution)/shard_map/all_to_all | solution.py:364
  53.5 1.0 %gather.1 = f32[32,3,8,128]{3,2,1,0:T(8,128)S(1)} custom-call(s32[64]{0:T(128)S(1)} %sources.1, f32[32,3,8,128]{3,2,1,0:T(8,128)S(1)} %all_to_all.10.before), custom_call_target="tpu_custom_call" | custom-call | tf_op jit(solution)/shard_map/gather/pallas_call | solution.py:276
  54.5 20.7 %all_to_all.11.arrived = f32[32,3,8,128]{3,2,1,0:T(8,128)S(1)} all-to-all(f32[32,3,8,128]{3,2,1,0:T(8,128)S(1)} %gather.1), channel_id=1, replica_groups=mesh['member'=32,'row'=8] {'member'}, dimensions={0} | all-to-all | bytes 786432 | tf_op jit(solution)/shard_map/all_to_all | solution.py:368
  75.2 2.0 %unpack.1 = f32[2,3,16,1024]{3,2,1,0:T(8,128)} custom-call(f32[32,3,8,128]{3,2,1,0:T(8,128)S(1)} %all_to_all.11.arrived), custom_call_target="tpu_custom_call" | custom-call | tf_op jit(solution)/shard_map/unpack/pallas_call | solution.py:369
Async XLA Ops:
  0.0 6.9 %copy-start = (s32[3,6,64]{2,1,0:T(8,128)S(1)}, s32[3,6,64]{2,1,0:T(8,128)}, u32[]{:S(2)}) copy-start(s32[3,6,64]{2,1,0:T(8,128)} %param.5) | copy-start | bytes 13828
  1.9 7.9 %collective-permute-start = (f32[4,8,1024]{2,1,0:T(8,128)S(1)}, f32[4,8,1024]{2,1,0:T(8,128)S(1)}, u32[]{:S(2)}, u32[]{:S(2)}) collective-permute-start(f32[4,8,1024]{2,1,0:T(8,128)S(1)} %get-tuple-element.22.own_outer), channel_id=1, source_target_pairs={{0,7},{1,2},{2,1},{3,4},{4,3},{5,6},{6,5},{7,0},{8,15},{9,10},{10,... | collective-permute-start | bytes 393224 | tf_op jit(solution)/shard_map/ppermute | solution.py:287
  6.1 3.7 %collective-permute-start.1 = (f32[4,8,1024]{2,1,0:T(8,128)S(1)}, f32[4,8,1024]{2,1,0:T(8,128)S(1)}, u32[]{:S(2)}, u32[]{:S(2)}) collective-permute-start(f32[4,8,1024]{2,1,0:T(8,128)S(1)} %get-tuple-element.23.own_inner), channel_id=1, source_target_pairs={{0,1},{1,0},{2,3},{3,2},{4,5},{5,4},{6,7},{7,6},{8,9},{9,8},{10,11... | collective-permute-start | bytes 393224 | tf_op jit(solution)/shard_map/ppermute | solution.py:287
  6.1 8.5 %collective-permute-start.2 = (f32[4,8,1024]{2,1,0:T(8,128)S(1)}, f32[4,8,1024]{2,1,0:T(8,128)S(1)}, u32[]{:S(2)}, u32[]{:S(2)}) collective-permute-start(f32[4,8,1024]{2,1,0:T(8,128)S(1)} %get-tuple-element.26.own_outer), channel_id=1, source_target_pairs={{0,7},{1,2},{2,1},{3,4},{4,3},{5,6},{6,5},{7,0},{8,15},{9,10},{10,... | collective-permute-start | bytes 393224 | tf_op jit(solution)/shard_map/ppermute | solution.py:287
  6.9 7.7 %collective-permute-start.3 = (f32[4,8,1024]{2,1,0:T(8,128)S(1)}, f32[4,8,1024]{2,1,0:T(8,128)S(1)}, u32[]{:S(2)}, u32[]{:S(2)}) collective-permute-start(f32[4,8,1024]{2,1,0:T(8,128)S(1)} %get-tuple-element.27.own_inner), channel_id=1, source_target_pairs={{0,1},{1,0},{2,3},{3,2},{4,5},{5,4},{6,7},{7,6},{8,9},{9,8},{10,11... | collective-permute-start | bytes 393224 | tf_op jit(solution)/shard_map/ppermute | solution.py:287
  10.8 9.2 %collective-permute-start.6 = (f32[3,16,1024]{2,1,0:T(8,128)S(1)}, f32[3,16,1024]{2,1,0:T(8,128)S(1)}, u32[]{:S(2)}, u32[]{:S(2)}) collective-permute-start(f32[3,16,1024]{2,1,0:T(8,128)S(1)} %get-tuple-element.30.own), channel_id=1, source_target_pairs={{0,7},{1,2},{2,1},{3,4},{4,3},{5,6},{6,5},{7,0},{8,15},{9,10},{10,... | collective-permute-start | bytes 589832 | tf_op jit(solution)/shard_map/ppermute | solution.py:287
  14.6 5.4 %collective-permute-start.7 = (f32[3,16,1024]{2,1,0:T(8,128)S(1)}, f32[3,16,1024]{2,1,0:T(8,128)S(1)}, u32[]{:S(2)}, u32[]{:S(2)}) collective-permute-start(f32[3,16,1024]{2,1,0:T(8,128)S(1)} %get-tuple-element.30.own), channel_id=1, source_target_pairs={{0,1},{1,0},{2,3},{3,2},{4,5},{5,4},{6,7},{7,6},{8,9},{9,8},{10,11... | collective-permute-start | bytes 589832 | tf_op jit(solution)/shard_map/ppermute | solution.py:287
  15.5 7.6 %collective-permute-start.4 = (f32[3,16,1024]{2,1,0:T(8,128)S(1)}, f32[3,16,1024]{2,1,0:T(8,128)S(1)}, u32[]{:S(2)}, u32[]{:S(2)}) collective-permute-start(f32[3,16,1024]{2,1,0:T(8,128)S(1)} %get-tuple-element.29.own), channel_id=1, source_target_pairs={{0,7},{1,2},{2,1},{3,4},{4,3},{5,6},{6,5},{7,0},{8,15},{9,10},{10,... | collective-permute-start | bytes 589832 | tf_op jit(solution)/shard_map/ppermute | solution.py:287
  16.0 7.1 %collective-permute-start.5 = (f32[3,16,1024]{2,1,0:T(8,128)S(1)}, f32[3,16,1024]{2,1,0:T(8,128)S(1)}, u32[]{:S(2)}, u32[]{:S(2)}) collective-permute-start(f32[3,16,1024]{2,1,0:T(8,128)S(1)} %get-tuple-element.29.own), channel_id=1, source_target_pairs={{0,1},{1,0},{2,3},{3,2},{4,5},{5,4},{6,7},{7,6},{8,9},{9,8},{10,11... | collective-permute-start | bytes 589832 | tf_op jit(solution)/shard_map/ppermute | solution.py:287

commit v4 on v2

--- a/solution.py
+++ b/solution.py
@@ -7,6 +7,7 @@
 from jax.experimental.pallas import tpu as pltpu
 from jax.sharding import PartitionSpec as P
 
+
 STEPS = 4
 HALO = 2 * STEPS
 LANES = 128
@@ -14,7 +15,6 @@
 HEIGHT_UNIT = 2.0**-5
 SPEED_UNIT = 2.0**-3
 
-gravity = 2.0
 coriolis = 0.1
 friction = 0.02
 time_step = 0.25
@@ -90,7 +90,7 @@
 
 
 def edge_kernel(odd, fields, bathymetry, *refs):
-    count, parts, rows, width = fields.shape
+    count, parts, _, _ = fields.shape
     outs, (held, held_depth, sems) = refs[: 2 * count], refs[2 * count :]
     copies = [pltpu.make_async_copy(bathymetry, held_depth, sems.at[count])]
     copies += [pltpu.make_async_copy(fields.at[m], held.at[m], sems.at[m]) for m in range(count)]
@@ -244,7 +244,7 @@
 
 
 def unpack_kernel(arrived, out):
-    count, _, rows, width = out.shape
+    _, _, _, width = out.shape
     blocks = width // LANES
     ways = arrived.shape[0] // blocks
     lane = lax.broadcasted_iota(jnp.int32, (HALO, LANES), 1)
@@ -271,7 +271,7 @@
     f32 = functools.partial(jax.ShapeDtypeStruct, dtype=jnp.float32)
     columns = f32((devices, parts, HALO, LANES))
 
-    def call(kernel, out_shape, *args, scratch=(), scalars=1, space=vmem, grant=16 << 20, name=None):
+    def call(kernel, out_shape, *args, scratch=(), scalars=1, space=vmem, grant=16 << 20):
         many = isinstance(out_shape, tuple)
         return pl.pallas_call(
             kernel,
@@ -280,7 +280,6 @@
             out_specs=(vmem,) * len(out_shape) if many else vmem,
             scratch_shapes=scratch,
             compiler_params=pltpu.CompilerParams(vmem_limit_bytes=grant),
-            name=name,
         )(*args)
 
     def exchange(outer, inner):
@@ -301,7 +300,6 @@
             pltpu.SemaphoreType.DMA((count + 1,)),
         ],
         space=pl.BlockSpec(memory_space=pltpu.HBM),
-        name="edge",
     )
     now = [edges[2 * m : 2 * m + 2] for m in range(count)]
     around = [exchange(*x) for x in now]
@@ -315,27 +313,19 @@
         compiler_params=pltpu.CompilerParams(vmem_limit_bytes=1 << 20),
         name="sources",
     )(copy_lists.reshape(-1))
-    pieces[0], sources = lax.optimization_barrier((pieces[0], sources))
 
     def state(tall):
         return [pltpu.VMEM((parts, blocks, tall, LANES), jnp.float32)]
 
     tall = rows + 2 * HALO
-    first, depth = call(
-        first_kernel, (tile, f32((blocks, tall, LANES))), odd, *pieces[0], scratch=state(tall), name="first"
-    )
+    first, depth = call(first_kernel, (tile, f32((blocks, tall, LANES))), odd, *pieces[0], scratch=state(tall))
     around = [exchange(first, first)]
     tall = rows * 3
     second, tall_depth = call(
-        second_kernel,
-        (tile, f32((blocks, tall, LANES))),
-        odd,
-        depth,
-        *pieces[1],
-        scratch=state(rows + 2 * HALO),
-        name="second",
+        second_kernel, (tile, f32((blocks, tall, LANES))), odd, depth, *pieces[1], scratch=state(rows + 2 * HALO)
     )
-    around.append(exchange(second, second))
+    beyond = lax.ppermute(second, "row", across_chips)
+    around.append((beyond, lax.ppermute(second, "row", within)))
     steps = (cycles - 1) * STEPS
     first = call(
         functools.partial(third_kernel, steps),
@@ -346,7 +336,6 @@
         first,
         around[0][1],
         scratch=state(tall),
-        name="third",
     )
     packed = call(
         functools.partial(last_kernel, steps),
@@ -358,13 +347,10 @@
         around[1][1],
         first,
         scratch=state(tall),
-        name="last",
     )
 
     own = lax.all_to_all(packed, "member", 0, 0, tiled=True)
-    chosen = call(
-        functools.partial(gather_kernel, width // devices), columns, sources, own, name="gather"
-    )
+    chosen = call(functools.partial(gather_kernel, width // devices), columns, sources, own)
     arrived = lax.all_to_all(chosen, "member", 0, 0, tiled=True)
     return pl.pallas_call(
         unpack_kernel,
@@ -379,6 +365,4 @@
 
 def solution(mesh):
     placed = (P("member", None, "row", None), P("row", None), P())
-    return jax.shard_map(
-        body, mesh=mesh, in_specs=placed, out_specs=P("member", None, "row", None), check_vma=False
-    )
+    return jax.shard_map(body, mesh=mesh, in_specs=placed, out_specs=P("member", None, "row", None), check_vma=False)

time: 77.3 us -> 78.5 us (1.016)
  blocking collectives: 47.4 us -> 21.2 us
  starting transfers between devices: 9.42 us -> 23.7 us
  waiting for transfers between devices: 5.08 us -> 17.4 us
    all_to_all x1 -> x0, blocking collectives: 27.1 us -> none  [body(): own = lax.all_to_all(packed, 'member', 0, 0, tiled=True)]
    all_to_all x0 -> x1, starting transfers between devices: none -> 13.2 us  [body(): own = lax.all_to_all(packed, 'member', 0, 0, tiled=True)]
    all_to_all x0 -> x1, waiting for transfers between devices: none -> 11.4 us  [body(): own = lax.all_to_all(packed, 'member', 0, 0, tiled=True)]
    ppermute x0 -> x2, starting transfers between devices: none -> 1.75 us  [the longest x1 1.75 us: body(): beyond = lax.ppermute(second, 'row', across_chips)]
    all_to_all x1, blocking collectives: 20.3 us -> 21.2 us  [body(): arrived = lax.all_to_all(chosen, 'member', 0, 0, tiled=True)]
    ppermute x4 -> x3, starting transfers between devices: 9.19 us -> 8.72 us  [exchange(): lax.ppermute(outer, 'row', across_chips)]
    ppermute x4 -> x3, waiting for transfers between devices: 5.07 us -> 5.39 us  [exchange(): lax.ppermute(outer, 'row', across_chips)]
  transfers between devices with their start and end apart: 8 -> 9, of which waited for: 3 -> 4; matrix products, arithmetic and copies ran while one was open for 0% -> 0% of each run, Pallas kernels for 9% -> 8%
where the time goes in v4:
time: 78.5 us; the launch traced here: 78.2 us
  starting transfers between devices  23.7 us (30%)
  blocking collectives  21.2 us (27%)
  waiting for transfers between devices  17.4 us (22%)
  Pallas kernels  15.8 us (20%)
    all_to_all x1, blocking collectives, body(): arrived = lax.all_to_all(chosen, 'member', 0, 0, tiled=True)  21.2 us
    all_to_all x1, starting transfers between devices, body(): own = lax.all_to_all(packed, 'member', 0, 0, tiled=True)  13.2 us
    pallas_call x6, Pallas kernels, call(): pl.pallas_call(kernel, out_shape=out_shape, in_specs=[smem] * scalars + [...  11.8 us
    all_to_all x1, waiting for transfers between devices, body(): own = lax.all_to_all(packed, 'member', 0, 0, tiled=True)  11.4 us
    ppermute x3, starting transfers between devices, exchange(): lax.ppermute(outer, 'row', across_chips)  8.72 us
    ppermute x3, waiting for transfers between devices, exchange(): lax.ppermute(outer, 'row', across_chips)  5.39 us
    pallas_call x1, Pallas kernels, body(): pl.pallas_call(source_kernel, out_shape=jax.ShapeDtypeStruct((count * dev...  2.02 us
    pallas_call x1, Pallas kernels, body(): pl.pallas_call(unpack_kernel, out_shape=f32(fields.shape), grid=(parts,),...  1.98 us
  transfers between devices with their start and end apart: 9, of which 4 were waited for; matrix products, arithmetic and copies ran while one was open for 0% of the time, Pallas kernels for 8%

profile of v4, /device:TPU:2, one launch (start us, length us, event | category | flops | bytes accessed | tf_op | source)
XLA Modules:
  0.0 78.2 jit_solution(7950037981347736485)
XLA Ops:
  0.0 1.9 %shard_map.37 = (f32[4,8,1024]{2,1,0:T(8,128)S(1)}, f32[4,8,1024]{2,1,0:T(8,128)S(1)}, f32[4,8,1024]{2,1,0:T(8,128)S(1)}, f32[4,8,1024]{2,1,0:T(8,128)S(1)}) custom-call(s32[1]{0:T(128)} %bitcast.odd, f32[2,3,16,1024]{3,2,1,0:T(8,128)} %fields.1, s32[16,1024]{1,0:T(8,128)} %bathymetry.1), custom_call_target="tpu_custom_call" | custom-call | tf_op jit(solution)/shard_map/pallas_call | solution.py:276
  1.9 4.2 %collective-permute-start = (f32[4,8,1024]{2,1,0:T(8,128)S(1)}, f32[4,8,1024]{2,1,0:T(8,128)S(1)}, u32[]{:S(2)}, u32[]{:S(2)}) collective-permute-start(f32[4,8,1024]{2,1,0:T(8,128)S(1)} %get-tuple-element.13.own_outer), channel_id=1, source_target_pairs={{0,7},{1,2},{2,1},{3,4},{4,3},{5,6},{6,5},{7,0},{8,15},{9,10},{10,... | collective-permute-start | bytes 393224 | tf_op jit(solution)/shard_map/ppermute | solution.py:286
  6.1 0.0 collective-permute-start.1
  6.1 0.8 collective-permute-start.2
  6.9 0.0 collective-permute-start.3
  6.9 2.9 %collective-permute-done.beyond = f32[4,8,1024]{2,1,0:T(8,128)S(1)} collective-permute-done((f32[4,8,1024]{2,1,0:T(8,128)S(1)}, f32[4,8,1024]{2,1,0:T(8,128)S(1)}, u32[]{:S(2)}, u32[]{:S(2)}) %collective-permute-start) | collective-permute-done | bytes 131104 | tf_op jit(solution)/shard_map/ppermute | solution.py:286
  9.8 0.0 collective-permute-done.1.beside
  9.8 0.9 %shard_map.38 = (f32[3,16,1024]{2,1,0:T(8,128)S(1)}, f32[8,32,128]{2,1,0:T(8,128)S(1)}) custom-call(s32[1]{0:T(128)} %bitcast.odd, f32[4,8,1024]{2,1,0:T(8,128)S(1)} %collective-permute-done.beyond, f32[4,8,1024]{2,1,0:T(8,128)S(1)} %get-tuple-element.13.own_outer, f32[4,8,1024]{2,1,0:T(8,128)S(1)} %get-tuple-element.14.own_inner, ...), custom_call_target="tpu_custom_call" | custom-call | tf_op jit(solution)/shard_map/pallas_call | solution.py:276
  10.8 3.8 %collective-permute-start.6 = (f32[3,16,1024]{2,1,0:T(8,128)S(1)}, f32[3,16,1024]{2,1,0:T(8,128)S(1)}, u32[]{:S(2)}, u32[]{:S(2)}) collective-permute-start(f32[3,16,1024]{2,1,0:T(8,128)S(1)} %get-tuple-element.20.own), channel_id=1, source_target_pairs={{0,7},{1,2},{2,1},{3,4},{4,3},{5,6},{6,5},{7,0},{8,15},{9,10},{10,... | collective-permute-start | bytes 589832 | tf_op jit(solution)/shard_map/ppermute | solution.py:286
  14.6 0.0 collective-permute-start.7
  14.6 0.0 collective-permute-done.2.beyond
  14.6 0.0 collective-permute-done.3.beside
  14.6 1.0 %shard_map.39 = (f32[3,16,1024]{2,1,0:T(8,128)S(1)}, f32[8,48,128]{2,1,0:T(8,128)S(1)}) custom-call(s32[1]{0:T(128)} %bitcast.odd, f32[8,32,128]{2,1,0:T(8,128)S(1)} %get-tuple-element.15.depth, f32[4,8,1024]{2,1,0:T(8,128)S(1)} %collective-permute-done.2.beyond, f32[4,8,1024]{2,1,0:T(8,128)S(1)} %get-tuple-element.16.own_outer, ...), custom_call_target="tpu_custom_call" | custom-call | tf_op jit(solution)/shard_map/pallas_call | solution.py:276
  15.5 1.7 %collective-permute-start.4 = (f32[3,16,1024]{2,1,0:T(8,128)S(1)}, f32[3,16,1024]{2,1,0:T(8,128)S(1)}, u32[]{:S(2)}, u32[]{:S(2)}) collective-permute-start(f32[3,16,1024]{2,1,0:T(8,128)S(1)} %get-tuple-element.19.own), channel_id=1, source_target_pairs={{0,7},{1,2},{2,1},{3,4},{4,3},{5,6},{6,5},{7,0},{8,15},{9,10},{10,... | collective-permute-start | bytes 589832 | tf_op jit(solution)/shard_map/ppermute | solution.py:327
  17.3 0.0 collective-permute-start.5
  17.3 2.5 %collective-permute-done.6.beyond = f32[3,16,1024]{2,1,0:T(8,128)S(1)} collective-permute-done((f32[3,16,1024]{2,1,0:T(8,128)S(1)}, f32[3,16,1024]{2,1,0:T(8,128)S(1)}, u32[]{:S(2)}, u32[]{:S(2)}) %collective-permute-start.6) | collective-permute-done | bytes 196640 | tf_op jit(solution)/shard_map/ppermute | solution.py:286
  19.7 0.0 collective-permute-done.7.beside
  19.7 2.7 %shard_map.40.other = f32[3,16,1024]{2,1,0:T(8,128)S(1)} custom-call(s32[1]{0:T(128)} %bitcast.odd, f32[8,48,128]{2,1,0:T(8,128)S(1)} %get-tuple-element.18.depth, f32[3,16,1024]{2,1,0:T(8,128)S(1)} %collective-permute-done.6.beyond, f32[3,16,1024]{2,1,0:T(8,128)S(1)} %get-tuple-element.20.own, f32[3,16,1024]{2,1,0:T(8,128)S(1)} %collective-permute-done.7.beside), custom_call_target="tpu_custom_call" | custom-call | tf_op jit(solution)/shard_map/pallas_call | solution.py:276
  22.4 0.6 collective-permute-done.4.beyond
  23.0 0.0 collective-permute-done.5.beside
  23.0 4.3 %shard_map.41 = f32[32,3,8,128]{3,2,1,0:T(8,128)} custom-call(s32[1]{0:T(128)} %bitcast.odd, f32[8,48,128]{2,1,0:T(8,128)S(1)} %get-tuple-element.18.depth, f32[3,16,1024]{2,1,0:T(8,128)S(1)} %collective-permute-done.4.beyond, f32[3,16,1024]{2,1,0:T(8,128)S(1)} %get-tuple-element.19.own, f32[3,16,1024]{2,1,0:T(8,128)S(1)} %collective-permute-done.5.beside, ...), custom_call_target="tpu_custom_call" | custom-call | tf_op jit(solution)/shard_map/pallas_call | solution.py:276
  27.3 0.0 copy-start
  27.3 13.2 %all-to-all-start = ((f32[32,3,8,128]{3,2,1,0:T(8,128)}), f32[32,3,8,128]{3,2,1,0:T(8,128)S(1)}, u32[]{:S(2)}, u32[]{:S(2)}) async-start(f32[32,3,8,128]{3,2,1,0:T(8,128)} %shard_map.41), calls=%async_computation | async-start | bytes 786432 | tf_op jit(solution)/shard_map/all_to_all | solution.py:352
  40.5 0.0 copy-done
  40.5 0.1 reshape.6.lists
  40.6 2.0 %sources.1 = s32[64]{0:T(128)S(1)} custom-call(s32[1152]{0:T(1024)S(1)} %reshape.6.lists), custom_call_target="tpu_custom_call" | custom-call | tf_op jit(solution)/shard_map/sources/pallas_call | solution.py:308
  42.6 11.4 %all-to-all-done.before = f32[32,3,8,128]{3,2,1,0:T(8,128)S(1)} async-done(((f32[32,3,8,128]{3,2,1,0:T(8,128)}), f32[32,3,8,128]{3,2,1,0:T(8,128)S(1)}, u32[]{:S(2)}, u32[]{:S(2)}) %all-to-all-start) | async-done | bytes 393248 | tf_op jit(solution)/shard_map/all_to_all | solution.py:352
  54.0 1.0 %shard_map.42 = f32[32,3,8,128]{3,2,1,0:T(8,128)S(1)} custom-call(s32[64]{0:T(128)S(1)} %sources.1, f32[32,3,8,128]{3,2,1,0:T(8,128)S(1)} %all-to-all-done.before), custom_call_target="tpu_custom_call" | custom-call | tf_op jit(solution)/shard_map/pallas_call | solution.py:276
  55.0 21.2 %all_to_all.10.arrived = f32[32,3,8,128]{3,2,1,0:T(8,128)S(1)} all-to-all(f32[32,3,8,128]{3,2,1,0:T(8,128)S(1)} %shard_map.42), channel_id=1, replica_groups=mesh['member'=32,'row'=8] {'member'}, dimensions={0} | all-to-all | bytes 786432 | tf_op jit(solution)/shard_map/all_to_all | solution.py:354
  76.2 2.0 %unpack.1 = f32[2,3,16,1024]{3,2,1,0:T(8,128)} custom-call(f32[32,3,8,128]{3,2,1,0:T(8,128)S(1)} %all_to_all.10.arrived), custom_call_target="tpu_custom_call" | custom-call | tf_op jit(solution)/shard_map/unpack/pallas_call | solution.py:355
Async XLA Ops:
  1.9 7.9 %collective-permute-start = (f32[4,8,1024]{2,1,0:T(8,128)S(1)}, f32[4,8,1024]{2,1,0:T(8,128)S(1)}, u32[]{:S(2)}, u32[]{:S(2)}) collective-permute-start(f32[4,8,1024]{2,1,0:T(8,128)S(1)} %get-tuple-element.13.own_outer), channel_id=1, source_target_pairs={{0,7},{1,2},{2,1},{3,4},{4,3},{5,6},{6,5},{7,0},{8,15},{9,10},{10,... | collective-permute-start | bytes 393224 | tf_op jit(solution)/shard_map/ppermute | solution.py:286
  6.1 3.7 %collective-permute-start.1 = (f32[4,8,1024]{2,1,0:T(8,128)S(1)}, f32[4,8,1024]{2,1,0:T(8,128)S(1)}, u32[]{:S(2)}, u32[]{:S(2)}) collective-permute-start(f32[4,8,1024]{2,1,0:T(8,128)S(1)} %get-tuple-element.14.own_inner), channel_id=1, source_target_pairs={{0,1},{1,0},{2,3},{3,2},{4,5},{5,4},{6,7},{7,6},{8,9},{9,8},{10,11... | collective-permute-start | bytes 393224 | tf_op jit(solution)/shard_map/ppermute | solution.py:286
  6.1 8.5 %collective-permute-start.2 = (f32[4,8,1024]{2,1,0:T(8,128)S(1)}, f32[4,8,1024]{2,1,0:T(8,128)S(1)}, u32[]{:S(2)}, u32[]{:S(2)}) collective-permute-start(f32[4,8,1024]{2,1,0:T(8,128)S(1)} %get-tuple-element.16.own_outer), channel_id=1, source_target_pairs={{0,7},{1,2},{2,1},{3,4},{4,3},{5,6},{6,5},{7,0},{8,15},{9,10},{10,... | collective-permute-start | bytes 393224 | tf_op jit(solution)/shard_map/ppermute | solution.py:286
  6.9 7.7 %collective-permute-start.3 = (f32[4,8,1024]{2,1,0:T(8,128)S(1)}, f32[4,8,1024]{2,1,0:T(8,128)S(1)}, u32[]{:S(2)}, u32[]{:S(2)}) collective-permute-start(f32[4,8,1024]{2,1,0:T(8,128)S(1)} %get-tuple-element.17.own_inner), channel_id=1, source_target_pairs={{0,1},{1,0},{2,3},{3,2},{4,5},{5,4},{6,7},{7,6},{8,9},{9,8},{10,11... | collective-permute-start | bytes 393224 | tf_op jit(solution)/shard_map/ppermute | solution.py:286
  10.8 9.0 %collective-permute-start.6 = (f32[3,16,1024]{2,1,0:T(8,128)S(1)}, f32[3,16,1024]{2,1,0:T(8,128)S(1)}, u32[]{:S(2)}, u32[]{:S(2)}) collective-permute-start(f32[3,16,1024]{2,1,0:T(8,128)S(1)} %get-tuple-element.20.own), channel_id=1, source_target_pairs={{0,7},{1,2},{2,1},{3,4},{4,3},{5,6},{6,5},{7,0},{8,15},{9,10},{10,... | collective-permute-start | bytes 589832 | tf_op jit(solution)/shard_map/ppermute | solution.py:286
  14.6 5.2 %collective-permute-start.7 = (f32[3,16,1024]{2,1,0:T(8,128)S(1)}, f32[3,16,1024]{2,1,0:T(8,128)S(1)}, u32[]{:S(2)}, u32[]{:S(2)}) collective-permute-start(f32[3,16,1024]{2,1,0:T(8,128)S(1)} %get-tuple-element.20.own), channel_id=1, source_target_pairs={{0,1},{1,0},{2,3},{3,2},{4,5},{5,4},{6,7},{7,6},{8,9},{9,8},{10,11... | collective-permute-start | bytes 589832 | tf_op jit(solution)/shard_map/ppermute | solution.py:286
  15.5 7.5 %collective-permute-start.4 = (f32[3,16,1024]{2,1,0:T(8,128)S(1)}, f32[3,16,1024]{2,1,0:T(8,128)S(1)}, u32[]{:S(2)}, u32[]{:S(2)}) collective-permute-start(f32[3,16,1024]{2,1,0:T(8,128)S(1)} %get-tuple-element.19.own), channel_id=1, source_target_pairs={{0,7},{1,2},{2,1},{3,4},{4,3},{5,6},{6,5},{7,0},{8,15},{9,10},{10,... | collective-permute-start | bytes 589832 | tf_op jit(solution)/shard_map/ppermute | solution.py:327
  17.3 5.7 %collective-permute-start.5 = (f32[3,16,1024]{2,1,0:T(8,128)S(1)}, f32[3,16,1024]{2,1,0:T(8,128)S(1)}, u32[]{:S(2)}, u32[]{:S(2)}) collective-permute-start(f32[3,16,1024]{2,1,0:T(8,128)S(1)} %get-tuple-element.19.own), channel_id=1, source_target_pairs={{0,1},{1,0},{2,3},{3,2},{4,5},{5,4},{6,7},{7,6},{8,9},{9,8},{10,11... | collective-permute-start | bytes 589832 | tf_op jit(solution)/shard_map/ppermute | solution.py:328
  27.3 13.2 %copy-start = (s32[3,6,64]{2,1,0:T(8,128)S(1)}, s32[3,6,64]{2,1,0:T(8,128)}, u32[]{:S(2)}) copy-start(s32[3,6,64]{2,1,0:T(8,128)} %param.5) | copy-start | bytes 13828
  27.3 26.7 %all-to-all-start = ((f32[32,3,8,128]{3,2,1,0:T(8,128)}), f32[32,3,8,128]{3,2,1,0:T(8,128)S(1)}, u32[]{:S(2)}, u32[]{:S(2)}) async-start(f32[32,3,8,128]{3,2,1,0:T(8,128)} %shard_map.41), calls=%async_computation | async-start | bytes 786432 | tf_op jit(solution)/shard_map/all_to_all | solution.py:352
